TPU v7x, 128 devices: a whole 4x4x4 slice. The times are simulated.
128 devices in a mesh: gx: 16 (over z, y), gy: 8 (over x, core).
Axes of the slice: x: 4, y: 4, z: 4, core: 2. Of those that a mesh axis runs over, the one named last changes fastest.
Arguments:
- density: float32 [512, 256, 512], P('gx', 'gy'), may hold values from 0.5 to 2
- momentum: float32 [3, 512, 256, 512], P(None, 'gx', 'gy'), may hold values from -3 to 3
- energy: float32 [512, 256, 512], P('gx', 'gy'), may hold values from 2 to 4
- coarse_rows: float32 [2, 4096, 8, 160], P(None, 'gx', 'gy'), may hold values from -2 to 4, as said below
- ghost_rows: int32 [8, 16, 128], P('gy'), may hold values from 0 to 4095, as said below
- time_index: int32 [8, 16, 128], P('gy'), may hold values from 0 to 8
Outputs:
- section_state: float32 [5, 512, 256, 512], P(None, 'gx', 'gy')
Inputs may be any that keep to these rules, and one draw needn't show every extreme that they name: `ghost_rows`: entry [b, a, s] names a coarse row of column b; rows c * 256 to (c + 1) * 256 - 1 of a column lie on the device with gx index c. Exactly 8 of one device's slots name rows held by each source device. `coarse_rows`: field 0 of every row (density) lies in 0.5 to 2.
All inputs are finite; a program needn't handle non-finite values.
Results may differ from a plain program's by a relative error of at most 0.0003.
Values sent between devices are 32-bit elements; how exact they have to be, the bound alone decides.
No kernel may reach another device: no remote copies, remote signals or barrier semaphores. Data moves between devices by JAX's collectives and lax.ppermute only.
A program may use at most 256 MiB of HBM per device.

v0:
```python
import math

import jax
import jax.numpy as jnp
from jax import lax
from jax.sharding import PartitionSpec as P

beta_coef = 1.0 / 3.0
a_coef = 14.0 / 9.0
b_coef = 1.0 / 9.0
gamma_gas = 1.4
time_step = 0.4
root_scale = math.sqrt(1.0 - 4.0 * beta_coef * beta_coef)
root_value = (-1.0 + root_scale) / (2.0 * beta_coef)
root_log = math.log(-root_value)
highest = lax.Precision.HIGHEST


def with_halo(block, sides, width):
    for axis, dim in sides:
        count = lax.axis_size(axis)
        forward = [(i, i + 1) for i in range(count - 1)]
        backward = [(target, source) for source, target in forward]
        low = lax.ppermute(
            lax.slice_in_dim(block, block.shape[dim] - width, None, axis=dim), axis, forward
        )
        high = lax.ppermute(lax.slice_in_dim(block, 0, width, axis=dim), axis, backward)
        block = jnp.concatenate([low, block, high], axis=dim)
    return block


def from_behind(array, axis, by):
    peers = lax.axis_size(axis)
    pairs = [(i, i + by) for i in range(peers) if 0 <= i + by < peers]
    return lax.ppermute(array, axis, pairs)


def fluxes(fields, direction):
    density = fields[0]
    carried = fields[1 + direction]
    velocity = carried / density
    kinetic = (fields[1] * fields[1] + fields[2] * fields[2] + fields[3] * fields[3]) / density
    pressure = (gamma_gas - 1.0) * (fields[4] - 0.5 * kinetic)
    columns = [carried]
    for component in range(3):
        product_term = fields[1 + component] * velocity
        if component == direction:
            product_term = product_term + pressure
        columns.append(product_term)
    columns.append((fields[4] + pressure) * velocity)
    return jnp.stack(columns)


def stencil(extended, line_axis, length):

    def window(offset):
        return lax.slice_in_dim(extended, offset, offset + length, axis=line_axis)

    return 0.5 * a_coef * (window(3) - window(1)) + 0.25 * b_coef * (window(4) - window(0))


def root_power(exponent):
    exponent = jnp.asarray(exponent, jnp.int32)
    signs = (1 - 2 * (exponent % 2)).astype(jnp.float32)
    return signs * jnp.exp(exponent.astype(jnp.float32) * root_log)


def inverse_entry(row_index, col_index, length):
    inside = (row_index >= 0) & (row_index < length) & (col_index >= 0) & (col_index < length)
    row_safe = jnp.clip(row_index, 0, length - 1)
    col_safe = jnp.clip(col_index, 0, length - 1)
    smaller = jnp.minimum(row_safe, col_safe)
    larger = jnp.maximum(row_safe, col_safe)
    entry_value = (
        root_power(larger - smaller)
        * (1.0 - root_power(2 * smaller + 2))
        * (1.0 - root_power(2 * (length - larger)))
    )
    entry_value = entry_value / (root_scale * (1.0 - root_power(2 * length + 2)))
    return jnp.where(inside, entry_value, 0.0)


def local_inverse(length):
    positions = jnp.arange(length, dtype=jnp.int32)
    return inverse_entry(positions[:, None], positions[None, :], length)


def edge_flux(extended, direction, line_axis, place, cells_side, length):
    positions = place * cells_side - 2 + jnp.arange(cells_side + 4, dtype=jnp.int32)
    valid = (positions >= 0) & (positions < length)
    shape = [1, 1, 1, 1]
    shape[line_axis] = cells_side + 4
    valid = valid.reshape(shape)
    safe = jnp.where(valid, extended, 1.0)
    return jnp.where(valid, fluxes(safe, direction), 0.0)


def add_interfaces(running, portion, first_block, device, cells_side, length):
    blocks = first_block + jnp.arange(portion.shape[0], dtype=jnp.int32)
    last_prev = device * cells_side - 1
    first_next = (device + 1) * cells_side
    before_rows = blocks * cells_side - 1
    after_rows = (blocks + 1) * cells_side
    coef_head_prev = -beta_coef * inverse_entry(last_prev, before_rows, length)
    coef_tail_prev = -beta_coef * inverse_entry(last_prev, after_rows, length) + (
        blocks == device - 1
    ).astype(jnp.float32)
    coef_head_next = -beta_coef * inverse_entry(first_next, before_rows, length) + (
        blocks == device + 1
    ).astype(jnp.float32)
    coef_tail_next = -beta_coef * inverse_entry(first_next, after_rows, length)
    head_values = portion[:, 0]
    tail_values = portion[:, 1]
    previous = (
        running[0]
        + jnp.einsum("j,jfoz->foz", coef_head_prev, head_values, precision=highest)
        + jnp.einsum("j,jfoz->foz", coef_tail_prev, tail_values, precision=highest)
    )
    following = (
        running[1]
        + jnp.einsum("j,jfoz->foz", coef_head_next, head_values, precision=highest)
        + jnp.einsum("j,jfoz->foz", coef_tail_next, tail_values, precision=highest)
    )
    return (previous, following)


def local(density, momentum, energy, coarse_rows, ghost_rows, time_index):
    fields = jnp.concatenate([density[None], momentum, energy[None]], axis=0)
    cells_side = density.shape[0]
    cells_z = density.shape[2]
    groups_x = lax.axis_size("gx")
    groups_y = lax.axis_size("gy")
    place_x = lax.axis_index("gx")
    place_y = lax.axis_index("gy")
    capacity = 4 * cells_side // groups_x
    coarse_block = coarse_rows.shape[1]
    slot_rows = ghost_rows[0]
    weights_all = time_index[0].astype(jnp.float32) * 0.125
    slot_used = slot_rows >= 0
    owners = jnp.where(slot_used, slot_rows // coarse_block, -1)
    from_self = (slot_used & (owners == place_x)).astype(jnp.int32)
    slot_rank = jnp.cumsum(from_self, axis=1) - 1
    positions = jnp.arange(capacity, dtype=jnp.int32)
    selector = from_self[:, None, :] * (slot_rank[:, None, :] == positions[None, :, None]).astype(
        jnp.int32
    )
    local_rows = jnp.sum(selector * (slot_rows - place_x * coarse_block)[:, None, :], axis=2)
    filled = jnp.sum(selector, axis=2) > 0
    flat_rows = jnp.where(filled, local_rows, 0).reshape(-1)
    level_old = jnp.where(
        filled[:, :, None], coarse_rows[0, :, 0, :][flat_rows].reshape(groups_x, capacity, -1), 0.0
    )
    level_new = jnp.where(
        filled[:, :, None], coarse_rows[1, :, 0, :][flat_rows].reshape(groups_x, capacity, -1), 0.0
    )
    own_rows = lax.dynamic_index_in_dim(slot_rows, place_x, 0, keepdims=False)
    own_weight = lax.dynamic_index_in_dim(weights_all, place_x, 0, keepdims=False)[:, None]
    own_used = own_rows >= 0
    own_owner = jnp.where(own_used, own_rows // coarse_block, -1)
    sources = jnp.arange(groups_x, dtype=jnp.int32)
    matches = (own_owner[None, :] == sources[:, None]).astype(jnp.int32)
    arrival_rank = jnp.sum(matches * jnp.cumsum(matches, axis=1), axis=0) - 1
    slot_index = jnp.where(own_used, own_owner * capacity + arrival_rank, 0)
    paired = jnp.stack([level_old, level_new], axis=1)
    received = lax.all_to_all(paired, "gx", split_axis=0, concat_axis=0, tiled=True)
    arrived_old = received[:, 0].reshape(groups_x * capacity, -1)[slot_index]
    arrived_new = received[:, 1].reshape(groups_x * capacity, -1)[slot_index]
    ghosts = (1.0 - own_weight) * arrived_old + own_weight * arrived_new
    ghosts = jnp.where(own_used[:, None], ghosts, 0.0).reshape(2, 2, cells_side, 5, cells_side)
    below_z = ghosts[0].transpose(2, 1, 3, 0)
    above_z = ghosts[1].transpose(2, 1, 3, 0)
    length_x = cells_side * groups_x
    length_y = cells_side * groups_y
    rimmed = with_halo(fields, (("gx", 1), ("gy", 2)), 2)
    extended_x = jnp.concatenate([rimmed[:, 0:2, 2:-2], fields, rimmed[:, -2:, 2:-2]], axis=1)
    extended_y = jnp.concatenate([rimmed[:, 2:-2, 0:2], fields, rimmed[:, 2:-2, -2:]], axis=2)
    extended_z = jnp.concatenate([below_z, fields, above_z], axis=3)
    block_inverse = local_inverse(cells_side)
    right_x = stencil(edge_flux(extended_x, 0, 1, place_x, cells_side, length_x), 1, cells_side)
    right_y = stencil(edge_flux(extended_y, 1, 2, place_y, cells_side, length_y), 2, cells_side)
    local_x = jnp.einsum("ij,fjyz->fiyz", block_inverse, right_x, precision=highest)
    local_y = jnp.einsum("ij,fxjz->fxiz", block_inverse, right_y, precision=highest)
    bounds_x = jnp.stack([local_x[:, 0], local_x[:, -1]], axis=0)[None]
    bounds_y = jnp.stack([local_y[:, :, 0], local_y[:, :, -1]], axis=0)[None]
    zeros_x = (
        jnp.zeros(bounds_x.shape[2:], jnp.float32),
        jnp.zeros(bounds_x.shape[2:], jnp.float32),
    )
    zeros_y = (
        jnp.zeros(bounds_y.shape[2:], jnp.float32),
        jnp.zeros(bounds_y.shape[2:], jnp.float32),
    )

    def fold_x(running, portion, first_block):
        return add_interfaces(running, portion, first_block, place_x, cells_side, length_x)

    def fold_y(running, portion, first_block):
        return add_interfaces(running, portion, first_block, place_y, cells_side, length_y)

    below_x = from_behind(bounds_x, "gx", 1)
    above_x = from_behind(bounds_x, "gx", -1)
    below_y = from_behind(bounds_y, "gy", 1)
    above_y = from_behind(bounds_y, "gy", -1)
    pair_x = fold_x(
        fold_x(fold_x(zeros_x, below_x, place_x - 1), bounds_x, place_x), above_x, place_x + 1
    )
    pair_y = fold_y(
        fold_y(fold_y(zeros_y, below_y, place_y - 1), bounds_y, place_y), above_y, place_y + 1
    )
    coupling_first = beta_coef * block_inverse[:, 0]
    coupling_last = beta_coef * block_inverse[:, -1]
    deriv_x = (
        local_x
        - coupling_first[None, :, None, None] * pair_x[0][:, None]
        - coupling_last[None, :, None, None] * pair_x[1][:, None]
    )
    deriv_y = (
        local_y
        - coupling_first[None, None, :, None] * pair_y[0][:, :, None]
        - coupling_last[None, None, :, None] * pair_y[1][:, :, None]
    )
    right_z = stencil(fluxes(extended_z, 2), 3, cells_z)
    deriv_z = jnp.dot(
        right_z.reshape(-1, cells_z), local_inverse(cells_z), precision=highest
    ).reshape(right_z.shape)
    return fields - time_step * (deriv_x + deriv_y + deriv_z)


def solution(mesh):
    return jax.shard_map(
        local,
        mesh=mesh,
        in_specs=(
            P("gx", "gy", None),
            P(None, "gx", "gy", None),
            P("gx", "gy", None),
            P(None, "gx", "gy", None),
            P("gy", None, None),
            P("gy", None, None),
        ),
        out_specs=P(None, "gx", "gy", None),
        check_vma=False,
    )
```

profile of v0, /device:TPU:1, one launch (start us, length us, event | category | flops | bytes accessed | tf_op | source)
XLA Modules:
  0.0 310.0 jit_solution(6944121693384401001)
XLA Ops:
  0.0 10.6 %pad_maximum_fusion.2 = f32[5,32,32,512]{3,2,0,1:T(8,128)} fusion(f32[1,32,32,512]{3,2,0,1:T(8,128)} %bitcast.236, f32[1,32,32,512]{3,2,0,1:T(8,128)} %bitcast.241, f32[3,32,32,512]{3,2,1,0:T(8,128)} %param.7), kind=kLoop, calls=%fused_computation.28 | loop fusion | flops 5242880 | bytes 20971520 | tf_op jit(solution)/shard_map/concatenate | solution.py:128
  10.6 2.4 fusion.178
  13.0 1.3 collective-permute-start.1
  14.3 5.5 %collective-permute-start = (f32[5,2,32,512]{3,2,0,1:T(8,128)S(1)}, f32[5,2,32,512]{3,2,0,1:T(8,128)}, u32[]{:S(2)}, u32[]{:S(2)}) collective-permute-start(f32[5,2,32,512]{3,2,0,1:T(8,128)S(1)} %get-tuple-element.30), channel_id=1, source_target_pairs={{0,8},{8,16},{16,24},{24,32},{32,40},{40,48},{48,56},{56,64},{64,7... | collective-permute-start | bytes 1966088 | tf_op jit(solution)/shard_map/ppermute | solution.py:24
  19.8 1.0 fusion.179
  24.5 9.0 %all-to-all-start = ((f32[16,2,8,160]{3,2,1,0:T(8,128)}), f32[16,2,8,160]{3,2,1,0:T(8,128)S(1)}, u32[]{:S(2)}, u32[]{:S(2)}) async-start(f32[16,2,8,160]{3,2,1,0:T(8,128)} %pad_maximum_fusion.3), calls=%async_computation | async-start | bytes 524288 | tf_op jit(solution)/shard_map/all_to_all | solution.py:165
  39.3 5.9 %all-to-all-done = f32[16,2,8,160]{3,2,1,0:T(8,128)S(1)} async-done(((f32[16,2,8,160]{3,2,1,0:T(8,128)}), f32[16,2,8,160]{3,2,1,0:T(8,128)S(1)}, u32[]{:S(2)}, u32[]{:S(2)}) %all-to-all-start) | async-done | bytes 163872 | tf_op jit(solution)/shard_map/all_to_all | solution.py:165
  47.0 2.5 copy.152
  49.6 2.5 copy.150
  52.2 9.5 %pad_maximum_fusion = f32[5,32,32,516]{3,2,0,1:T(8,128)S(1)} fusion(f32[5,32,32,2]{3,2,0,1:T(8,128)} %bitcast.247, f32[1,32,32,512]{3,2,0,1:T(8,128)S(1)} %bitcast.238, f32[1,32,32,512]{3,2,0,1:T(8,128)} %bitcast.242, f32[5,32,32,2]{3,2,0,1:T(8,128)} %bitcast.248, f32[3,32,32,512]{3,2,1,0:T(8,128)} %param.7), kind=kLoop, calls=%fused_computation.5 | loop fusion | flops 10567680 | bytes 21135360 | tf_op jit(solution)/shard_map/concatenate | solution.py:177
  62.6 5.1 %copy-done.6 = f32[5,32,32,516]{3,2,0,1:T(8,128)} copy-done((f32[5,32,32,516]{3,2,0,1:T(8,128)}, f32[5,32,32,516]{3,2,0,1:T(8,128)S(1)}, u32[]{:S(2)}) %copy-start.6) | copy-done | bytes 10567704
  67.7 1.9 multiply_dynamic-update-slice_fusion.1
  69.7 2.7 copy-done
  72.4 3.1 add_dynamic-update-slice_fusion
  75.5 8.9 %broadcast_select_fusion.2 = (f32[5,36,32,512]{3,2,0,1:T(8,128)S(1)}, f32[5,36,32,512]{3,2,0,1:T(8,128)}) fusion(pred[36]{0:T(512)(128)(4,1)S(1)} %compare_and_fusion.1, f32[5,2,32,512]{3,2,0,1:T(8,128)} %collective-permute-done.1, f32[1,32,32,512]{3,2,0,1:T(8,128)} %bitcast.237, f32[1,32,32,512]{3,2,0,1:T(8,128)} %bitcast.243, ...), kind=kLoop, calls=%fused_computation.35 | loop fusion | flops 14745600 | bytes 35389476 | tf_op jit(solution)/shard_map/jit(_where)/select_n | solution.py:94
  84.4 3.5 %fusion.176 = (f32[5,36,2,512]{3,2,0,1:T(2,128)S(1)}, f32[5,36,2,512]{3,2,0,1:T(2,128)S(1)}) fusion(f32[5,36,32,512]{3,2,0,1:T(8,128)} %get-tuple-element.23), kind=kLoop, calls=%fused_computation.283 | loop fusion | bytes 2949120 | tf_op jit(solution)/shard_map/slice | solution.py:25
  87.8 1.1 copy.134
  88.9 3.5 %collective-permute-start.4 = (f32[5,36,2,512]{3,2,1,0:T(2,128)}, f32[5,36,2,512]{3,2,1,0:T(2,128)}, u32[]{:S(2)}, u32[]{:S(2)}) collective-permute-start(f32[5,36,2,512]{3,2,1,0:T(2,128)} %copy.134), channel_id=1, source_target_pairs={{0,1},{1,2},{2,3},{3,4},{4,5},{5,6},{6,7},{8,9},{9,10},{10,11},{11... | collective-permute-start | bytes 2211848 | tf_op jit(solution)/shard_map/ppermute | solution.py:24
  92.4 1.1 copy.136
  93.6 2.1 collective-permute-start.5
  95.7 1.6 slice_dynamic-update-slice_fusion.2
  97.4 2.6 add_dynamic-update-slice_fusion.2
  100.0 2.1 multiply_dynamic-update-slice_fusion.8
  102.1 2.1 multiply_dynamic-update-slice_fusion.7
  104.1 2.3 multiply_dynamic-update-slice_fusion.6
  106.4 11.5 %broadcast_select_fusion.1 = f32[5,36,32,512]{3,2,0,1:T(8,128)} fusion(f32[5,36,32,512]{3,2,0,1:T(8,128)} %multiply_dynamic-update-slice_fusion.6, pred[36]{0:T(512)(128)(4,1)S(1)} %compare_and_fusion.1), kind=kLoop, calls=%fused_computation.34 | loop fusion | flops 2949120 | bytes 23592996 | tf_op jit(solution)/shard_map/jit(_where)/select_n | solution.py:95
  117.9 15.6 %fusion.17 = f32[5,32,32,512]{3,2,0,1:T(8,128)S(1)} fusion(f32[5,36,32,512]{3,2,0,1:T(8,128)} %broadcast_select_fusion.1), kind=kLoop, calls=%fused_computation.25 | loop fusion | flops 13107200 | bytes 52428800 | tf_op jit(solution)/shard_map/add | solution.py:59
  133.6 17.2 %fusion.19 = f32[5,32,512,32]{2,3,1,0:T(8,128)} fusion(f32[5,32,32,512]{3,2,0,1:T(8,128)S(1)} %fusion.17, s32[32]{0:T(128)S(1)} %iota_clamp_fusion.1, pred[32]{0:T(512)(128)(4,1)S(1)} %iota_compare_fusion.3), kind=kOutput, calls=%fused_computation.30 | convolution fusion | flops 1006699520 | bytes 20971680 | tf_op jit(solution)/shard_map/ij,fjyz->fiyz/dot_general | solution.py:181
  150.8 14.3 %copy.194 = f32[5,32,512,32]{2,1,0,3:T(8,128)} copy(f32[5,32,512,32]{2,3,1,0:T(8,128)} %fusion.19) | data formatting | bytes 20971520 | tf_op jit(solution)/shard_map/ij,fjyz->fiyz/dot_general | solution.py:181
  165.1 1.1 slice_bitcast_fusion.1
  166.3 1.3 collective-permute-start.3
  167.6 4.8 %collective-permute-start.2 = (f32[1,2,5,32,512]{4,3,2,1,0:T(8,128)S(1)}, f32[1,2,5,32,512]{4,3,2,1,0:T(8,128)}, u32[]{:S(2)}, u32[]{:S(2)}) collective-permute-start(f32[1,2,5,32,512]{4,3,2,1,0:T(8,128)S(1)} %maximum_bitcast_fusion), channel_id=1, source_target_pairs={{0,8},{8,16},{16,24},{24,32},{32,40},{40,48},{48,56},{56,64},{64,7... | collective-permute-start | bytes 1966088 | tf_op jit(solution)/shard_map/ppermute | solution.py:35
  172.4 4.4 %maximum_select_fusion = f32[5,32,36,512]{3,2,0,1:T(8,128)S(1)} fusion(f32[1,32,32,512]{3,2,0,1:T(8,128)S(1)} %bitcast.239, f32[1,32,32,512]{3,2,0,1:T(8,128)S(1)} %bitcast.245, pred[36]{0:T(512)(128)(4,1)S(1)} %compare_and_fusion, f32[5,36,2,512]{3,2,1,0:T(2,128)} %collective-permute-done.4, f32[5,36,2,512]{3,2,1,0:T(2,128)} %collective-permute-done.5, ...), kind=kLoop, calls=%fused_computation.4 | loop fusion | flops 14745600 | bytes 23592996 | tf_op jit(solution)/shard_map/jit(_where)/select_n | solution.py:94
  176.8 1.7 slice_dynamic-update-slice_fusion.1
  178.5 2.5 multiply_dynamic-update-slice_fusion.5
  181.1 3.1 %add_dynamic-update-slice_fusion.1 = (f32[5,32,36,512]{3,2,0,1:T(8,128)}, f32[1,32,36,512]{3,2,0,1:T(8,128)S(1)}) fusion(f32[5,32,36,512]{3,2,0,1:T(8,128)} %get-tuple-element.20, f32[1,32,36,512]{3,2,0,1:T(8,128)S(1)} %get-tuple-element.21, f32[5,32,36,512]{3,2,0,1:T(8,128)S(1)} %maximum_select_fusion), kind=kLoop, calls=%fused_computation.48 | loop fusion | flops 6488064 | bytes 19136512
  184.2 2.2 multiply_dynamic-update-slice_fusion.4
  186.4 2.4 multiply_dynamic-update-slice_fusion.3
  188.8 11.3 %broadcast_select_fusion = f32[5,32,36,512]{3,2,0,1:T(8,128)} fusion(f32[5,32,36,512]{3,2,0,1:T(8,128)} %multiply_dynamic-update-slice_fusion.3, pred[36]{0:T(512)(128)(4,1)S(1)} %compare_and_fusion), kind=kLoop, calls=%fused_computation.33 | loop fusion | flops 2949120 | bytes 23592996 | tf_op jit(solution)/shard_map/jit(_where)/select_n | solution.py:95
  200.1 29.7 %fusion.25 = f32[5,32,32,512]{3,2,0,1:T(8,128)} fusion(f32[5,32,36,512]{3,2,0,1:T(8,128)} %broadcast_select_fusion, s32[32]{0:T(128)S(1)} %iota_clamp_fusion.1, pred[32]{0:T(512)(128)(4,1)S(1)} %iota_compare_fusion.3), kind=kOutput, calls=%fused_computation.40 | convolution fusion | flops 1019806720 | bytes 52430848 | tf_op jit(solution)/shard_map/ij,fxjz->fxiz/dot_general | solution.py:182
  229.8 3.2 %fusion.177 = (f32[5,32,1,512]{3,2,0,1:T(1,128)S(1)}, f32[5,32,1,512]{3,2,0,1:T(1,128)S(1)}) fusion(f32[5,32,32,512]{3,2,0,1:T(8,128)} %fusion.25), kind=kLoop, calls=%fused_computation.284 | loop fusion | bytes 1310720 | tf_op jit(solution)/shard_map/slice | solution.py:184
  233.1 1.9 collective-permute-start.7
  235.0 4.2 %collective-permute-start.6 = (f32[1,2,5,32,512]{4,3,2,1,0:T(8,128)S(1)}, f32[1,2,5,32,512]{4,3,2,1,0:T(8,128)S(1)}, u32[]{:S(2)}, u32[]{:S(2)}) collective-permute-start(f32[1,2,5,32,512]{4,3,2,1,0:T(8,128)S(1)} %maximum_bitcast_fusion.1), channel_id=1, source_target_pairs={{0,1},{1,2},{2,3},{3,4},{4,5},{5,6},{6,7},{8,9},{9,10},{10,11},{11... | collective-permute-start | bytes 1966088 | tf_op jit(solution)/shard_map/ppermute | solution.py:35
  239.2 3.9 %multiply_dynamic-update-slice_fusion = f32[5,32,32,516]{3,2,0,1:T(8,128)} fusion(f32[5,32,32,516]{3,2,0,1:T(8,128)} %get-tuple-element.7, f32[1,32,32,516]{3,2,0,1:T(8,128)S(1)} %get-tuple-element.10, f32[1,32,32,516]{3,2,0,1:T(8,128)S(1)} %copy-done.5, f32[5,32,32,516]{3,2,0,1:T(8,128)} %copy-done), kind=kLoop, calls=%fused_computation.41 | loop fusion | flops 1056768 | bytes 9469952 | tf_op jit(solution)/shard_map/stack | solution.py:51
  243.2 2.4 add_bitcast_fusion.2
  245.5 2.2 add_bitcast_fusion.3
  248.7 50.6 %multiply_subtract_fusion = f32[5,32,32,512]{3,2,0,1:T(8,128)} fusion(f32[5,32,32,512]{3,2,0,1:T(8,128)} %fusion.25, f32[5,32,512]{2,0,1:T(8,128)S(1)} %copy.144, f32[32]{0:T(128)S(1)} %get-tuple-element.39, f32[5,32,512]{2,0,1:T(8,128)S(1)} %copy.143, f32[32]{0:T(128)S(1)} %get-tuple-element.38, f32[5,32,512]{2,1,0:T(8,128)} %add_bitcast_fusion.2, ...), kind=kOutput, calls=%fused_computation.32 | convolution fusion | flops 16172974080 | bytes 85597184 | tf_op jit(solution)/shard_map/dot_general | solution.py:223
  299.3 10.5 %copy.155 = f32[5,32,32,512]{3,2,1,0:T(8,128)} copy(f32[5,32,32,512]{3,2,0,1:T(8,128)} %multiply_subtract_fusion) | data formatting | bytes 20971520 | tf_op jit(solution)/shard_map/sub | solution.py:226
  (73 shorter events, 8.6 us)
Async XLA Ops:
  0.0 21.0 %copy-start.7 = (s32[1,16,128]{2,1,0:T(8,128)S(1)}, s32[1,16,128]{2,1,0:T(8,128)}, u32[]{:S(2)}) copy-start(s32[1,16,128]{2,1,0:T(8,128)} %param.10) | copy-start | bytes 24580
  10.6 41.6 %copy-start.1 = (f32[32,32,512]{2,1,0:T(8,128)S(1)}, f32[32,32,512]{2,1,0:T(8,128)}, u32[]{:S(2)}) copy-start(f32[32,32,512]{2,1,0:T(8,128)} %param.8) | copy-start | bytes 6291460
  13.0 62.5 %collective-permute-start.1 = (f32[5,2,32,512]{3,2,0,1:T(8,128)}, f32[5,2,32,512]{3,2,0,1:T(8,128)}, u32[]{:S(2)}, u32[]{:S(2)}) collective-permute-start(f32[5,2,32,512]{3,2,0,1:T(8,128)} %get-tuple-element.31), channel_id=1, source_target_pairs={{8,0},{16,8},{24,16},{32,24},{40,32},{48,40},{56,48},{64,56},{72,6... | collective-permute-start | bytes 1966088 | tf_op jit(solution)/shard_map/ppermute | solution.py:27
  14.3 61.2 %collective-permute-start = (f32[5,2,32,512]{3,2,0,1:T(8,128)S(1)}, f32[5,2,32,512]{3,2,0,1:T(8,128)}, u32[]{:S(2)}, u32[]{:S(2)}) collective-permute-start(f32[5,2,32,512]{3,2,0,1:T(8,128)S(1)} %get-tuple-element.30), channel_id=1, source_target_pairs={{0,8},{8,16},{16,24},{24,32},{32,40},{40,48},{48,56},{56,64},{64,7... | collective-permute-start | bytes 1966088 | tf_op jit(solution)/shard_map/ppermute | solution.py:24
  24.5 20.7 %all-to-all-start = ((f32[16,2,8,160]{3,2,1,0:T(8,128)}), f32[16,2,8,160]{3,2,1,0:T(8,128)S(1)}, u32[]{:S(2)}, u32[]{:S(2)}) async-start(f32[16,2,8,160]{3,2,1,0:T(8,128)} %pad_maximum_fusion.3), calls=%async_computation | async-start | bytes 524288 | tf_op jit(solution)/shard_map/all_to_all | solution.py:165
  61.7 10.7 %copy-start = (f32[5,32,32,516]{3,2,0,1:T(8,128)}, f32[5,32,32,516]{3,2,0,1:T(8,128)S(1)}, u32[]{:S(2)}) copy-start(f32[5,32,32,516]{3,2,0,1:T(8,128)S(1)} %pad_maximum_fusion) | copy-start | bytes 31703044
  62.6 5.1 %copy-start.6 = (f32[5,32,32,516]{3,2,0,1:T(8,128)}, f32[5,32,32,516]{3,2,0,1:T(8,128)S(1)}, u32[]{:S(2)}) copy-start(f32[5,32,32,516]{3,2,0,1:T(8,128)S(1)} %get-tuple-element.9) | copy-start | bytes 31703044
  67.7 7.8 %slice-start = ((s8[6291456]{0:T(1024)(128)(4,1)}), s8[4194304]{0:T(1024)(128)(4,1)S(1)}, s32[]{:S(2)}) async-start(s8[6291456]{0:T(1024)(128)(4,1)} %bitcast.234), calls=%async_computation.1 | async-start | bytes 8388608
  72.4 3.1 slice-start.1
  88.9 83.5 %collective-permute-start.4 = (f32[5,36,2,512]{3,2,1,0:T(2,128)}, f32[5,36,2,512]{3,2,1,0:T(2,128)}, u32[]{:S(2)}, u32[]{:S(2)}) collective-permute-start(f32[5,36,2,512]{3,2,1,0:T(2,128)} %copy.134), channel_id=1, source_target_pairs={{0,1},{1,2},{2,3},{3,4},{4,5},{5,6},{6,7},{8,9},{9,10},{10,11},{11... | collective-permute-start | bytes 2211848 | tf_op jit(solution)/shard_map/ppermute | solution.py:24
  93.6 78.8 %collective-permute-start.5 = (f32[5,36,2,512]{3,2,1,0:T(2,128)}, f32[5,36,2,512]{3,2,1,0:T(2,128)}, u32[]{:S(2)}, u32[]{:S(2)}) collective-permute-start(f32[5,36,2,512]{3,2,1,0:T(2,128)} %copy.136), channel_id=1, source_target_pairs={{1,0},{2,1},{3,2},{4,3},{5,4},{6,5},{7,6},{9,8},{10,9},{11,10},{12... | collective-permute-start | bytes 2211848 | tf_op jit(solution)/shard_map/ppermute | solution.py:27
  150.8 21.7 %copy-start.2 = (f32[32,32,512]{2,1,0:T(8,128)S(1)}, f32[32,32,512]{2,1,0:T(8,128)}, u32[]{:S(2)}) copy-start(f32[32,32,512]{2,1,0:T(8,128)} %param.8) | copy-start | bytes 6291460
  150.8 21.6 %copy-start.4 = (f32[32,32,512]{2,1,0:T(8,128)S(1)}, f32[32,32,512]{2,1,0:T(8,128)}, u32[]{:S(2)}) copy-start(f32[32,32,512]{2,1,0:T(8,128)} %param.6) | copy-start | bytes 6291460
  166.3 76.9 %collective-permute-start.3 = (f32[1,2,5,32,512]{4,3,2,1,0:T(8,128)S(1)}, f32[1,2,5,32,512]{4,3,2,1,0:T(8,128)}, u32[]{:S(2)}, u32[]{:S(2)}) collective-permute-start(f32[1,2,5,32,512]{4,3,2,1,0:T(8,128)S(1)} %maximum_bitcast_fusion), channel_id=1, source_target_pairs={{8,0},{16,8},{24,16},{32,24},{40,32},{48,40},{56,48},{64,56},{72,6... | collective-permute-start | bytes 1966088 | tf_op jit(solution)/shard_map/ppermute | solution.py:35
  167.6 75.6 %collective-permute-start.2 = (f32[1,2,5,32,512]{4,3,2,1,0:T(8,128)S(1)}, f32[1,2,5,32,512]{4,3,2,1,0:T(8,128)}, u32[]{:S(2)}, u32[]{:S(2)}) collective-permute-start(f32[1,2,5,32,512]{4,3,2,1,0:T(8,128)S(1)} %maximum_bitcast_fusion), channel_id=1, source_target_pairs={{0,8},{8,16},{16,24},{24,32},{32,40},{40,48},{48,56},{56,64},{64,7... | collective-permute-start | bytes 1966088 | tf_op jit(solution)/shard_map/ppermute | solution.py:35
  200.1 39.1 %copy-start.5 = (f32[1,32,32,516]{3,2,0,1:T(8,128)S(1)}, f32[1,32,32,516]{3,2,0,1:T(8,128)}, u32[]{:S(2)}) copy-start(f32[1,32,32,516]{3,2,0,1:T(8,128)} %get-tuple-element.8) | copy-start | bytes 6340612
  233.1 14.7 %collective-permute-start.7 = (f32[1,2,5,32,512]{4,3,2,1,0:T(8,128)S(1)}, f32[1,2,5,32,512]{4,3,2,1,0:T(8,128)S(1)}, u32[]{:S(2)}, u32[]{:S(2)}) collective-permute-start(f32[1,2,5,32,512]{4,3,2,1,0:T(8,128)S(1)} %maximum_bitcast_fusion.1), channel_id=1, source_target_pairs={{1,0},{2,1},{3,2},{4,3},{5,4},{6,5},{7,6},{9,8},{10,9},{11,10},{12... | collective-permute-start | bytes 1966088 | tf_op jit(solution)/shard_map/ppermute | solution.py:35
  235.0 12.8 %collective-permute-start.6 = (f32[1,2,5,32,512]{4,3,2,1,0:T(8,128)S(1)}, f32[1,2,5,32,512]{4,3,2,1,0:T(8,128)S(1)}, u32[]{:S(2)}, u32[]{:S(2)}) collective-permute-start(f32[1,2,5,32,512]{4,3,2,1,0:T(8,128)S(1)} %maximum_bitcast_fusion.1), channel_id=1, source_target_pairs={{0,1},{1,2},{2,3},{3,4},{4,5},{5,6},{6,7},{8,9},{9,10},{10,11},{11... | collective-permute-start | bytes 1966088 | tf_op jit(solution)/shard_map/ppermute | solution.py:35
  243.2 5.5 %copy-start.3 = (f32[32,32,512]{2,1,0:T(8,128)S(1)}, f32[32,32,512]{2,1,0:T(8,128)}, u32[]{:S(2)}) copy-start(f32[32,32,512]{2,1,0:T(8,128)} %param.8) | copy-start | bytes 6291460
where the time goes:
time: 314 us; the launch traced here: 310 us
  other arithmetic  109 us (35%)
  matrix products  97.5 us (31%)
  local copies, waits for them, and re-layouts  58.7 us (19%)
  starting transfers between devices  33.7 us (11%)
  waiting for transfers between devices  5.95 us (2%)
  between operations  5.17 us (2%)
    dot_general x1, matrix products, local(): jnp.dot(right_z.reshape(-1, cells_z), local_inverse(cells_z), precision=h...  50.6 us
    dot_general x1, matrix products, local(): jnp.einsum('ij,fxjz->fxiz', block_inverse, right_y, precision=highest)  29.7 us
    select_n x2, other arithmetic, edge_flux(): return jnp.where(valid, fluxes(safe, direction), 0.0)  22.8 us
    unnamed x10, other arithmetic  20.4 us
    dot_general x1, matrix products, local(): jnp.einsum('ij,fjyz->fiyz', block_inverse, right_x, precision=highest)  17.2 us
    add x1, other arithmetic, stencil(): 0.5 * a_coef * (window(3) - window(1))  15.6 us
    dot_general x1, local copies, waits for them, and re-layouts, local(): jnp.einsum('ij,fjyz->fiyz', block_inverse, right_x, precision=highest)  14.3 us
    select_n x2, other arithmetic, edge_flux(): safe = jnp.where(valid, extended, 1.0)  13.2 us
  transfers between devices with their start and end apart: 9, of which 1 were waited for; matrix products, arithmetic and copies ran while one was open for 54% of the time, Pallas kernels for 0%

commit v1 on v0

v1 whole, which is shorter than its diff:
```python
import functools
import math

import jax
import jax.numpy as jnp
import ml_dtypes
import numpy as np
from jax import lax
from jax.experimental import pallas as pl
from jax.experimental.pallas import tpu as pltpu
from jax.sharding import PartitionSpec as P

BETA = 1.0 / 3.0
NEAR = 7.0 / 9.0
FAR = 1.0 / 36.0
STEP = 0.4
KAPPA = math.sqrt(1.0 - 4.0 * BETA * BETA)
ROOT = (-1.0 + KAPPA) / (2.0 * BETA)
TAIL = (NEAR * (1.0 / ROOT - ROOT) + FAR * (1.0 / ROOT**2 - ROOT**2)) / KAPPA
FIRST = (NEAR * (1.0 - ROOT**2) + FAR * (ROOT - ROOT**3)) / KAPPA
SCALE = 1.253065
B = 32
NZ = 512
F32 = jnp.float32
BF16 = jnp.bfloat16
highest = lax.Precision.HIGHEST


@functools.cache
def derivative_matrix(length):
    extended = np.zeros((length, length + 4))
    rows = np.arange(length)
    extended[rows, rows + 3] += NEAR
    extended[rows, rows + 1] -= NEAR
    extended[rows, rows + 4] += FAR
    extended[rows, rows] -= FAR
    left = np.eye(length) + BETA * (np.eye(length, k=1) + np.eye(length, k=-1))
    return np.linalg.solve(left, extended)


def rounded(matrix):
    return np.asarray(matrix, np.float32).astype(ml_dtypes.bfloat16)


def block_matrix(outer):
    place = np.arange(B)
    gap = place[None, :] - place[:, None]
    size = np.abs(gap).astype(float)
    entry = np.where(size == 0, 0.0, np.where(size == 1, FIRST, TAIL * ROOT**size))

    def spread(part):
        part = np.kron(np.eye(8), part) if outer else np.kron(part, np.eye(8))
        part = part.reshape(-1, 32, 1, 8)
        return np.concatenate([part, part], axis=2).reshape(-1, 512)

    right, left = ROOT ** (B - 1.0 - place), ROOT ** (place * 1.0)
    rows = [spread(np.sign(gap) * entry * SCALE)]
    rows += [spread(w[None]).astype(np.float32) for w in (right, left)]
    rows += [spread((w - rounded(w).astype(float))[None]) for w in (right, left)]
    rows += [spread((place == at)[None] * 1.0) for at in (B - 1, 0)]
    return rounded(np.concatenate(rows, axis=0))


def z_matrix():
    return rounded(derivative_matrix(NZ)[:, 2:-2].T * SCALE)


def ghost_matrix():
    full = derivative_matrix(NZ)
    table = np.zeros((4, 256))
    table[0:2, :128] = full[:128, 0:2].T
    table[2:4, 128:] = full[-128:, -2:].T
    table = np.asarray(-STEP * np.repeat(table, 8, axis=0), np.float32)
    high = rounded(table)
    low = rounded(table - high.astype(np.float32))
    return np.concatenate([high, high, low], axis=0)


def edge_weights():
    place = np.arange(B)
    table = np.zeros((4, B))
    table[0] = STEP * TAIL * ROOT ** (place + 1.0)
    table[1, 0] = STEP * (FIRST - TAIL * ROOT)
    table[2] = -STEP * TAIL * ROOT ** (B - place * 1.0)
    table[3, -1] = -STEP * (FIRST - TAIL * ROOT)
    return table.astype(np.float32)


def state_parts(density, m1, m2, m3, energy):
    inverse = 1.0 / density
    u1, u2, u3 = m1 * inverse, m2 * inverse, m3 * inverse
    pressure = 0.4 * energy - 0.2 * (m1 * u1 + m2 * u2 + m3 * u3)
    return u1, u2, u3, pressure


def split(value):
    high = value.astype(BF16)
    return high, (value - high.astype(F32)).astype(BF16)


def halves(value):
    high = value.astype(BF16).astype(F32)
    both = jnp.concatenate([high, value - high], axis=1).astype(BF16)
    return both.reshape(-1, 128)


PIECES = 7
ANYWHERE = pl.BlockSpec(memory_space=pl.ANY)
IN_VMEM = pl.BlockSpec(memory_space=pltpu.VMEM)


def piece_slices(k):
    xs = 2 * (k // 8)
    yh = (k // 4) % 2
    ys = pl.ds(pl.multiple_of(16 * yh, 16), 16)
    zs = pl.ds(pl.multiple_of(128 * (k % 4), 128), 128)
    return xs, yh, ys, zs


def state_copies(rho, mom, ene, state, sems, i, first=0):
    xs = pl.ds(8 * (first + i), 8)
    to = pl.ds(8 * i, 8)
    return (
        pltpu.make_async_copy(rho.at[xs], state.at[0, to], sems.at[i, 0]),
        pltpu.make_async_copy(mom.at[:, xs], state.at[1:4, to], sems.at[i, 1]),
        pltpu.make_async_copy(ene.at[xs], state.at[4, to], sems.at[i, 2]),
    )


def xy_kernel(rho, mom, ene, kx, ky, after, part, xr, xl, yr, yl, fbuf, g0, g1, sems):
    factor = STEP / SCALE
    copies = [state_copies(rho, mom, ene, part, sems, i) for i in range(4)]
    for group in copies:
        for copy in group:
            copy.start()

    def piece(i, k, gbuf):
        xp, yh, ys, zs = piece_slices(k)
        xs = pl.ds(8 * i + xp, 2)
        d, m1, m2, m3, e = (part[c, xs, ys, zs].reshape(4, 8, 128) for c in range(5))
        u1, u2, u3, p = state_parts(d, m1, m2, m3, e)
        ep = e + p
        cross = halves(m1 * u2)
        f = (halves(m1), halves(m1 * u1 + p), cross, halves(m3 * u1), halves(ep * u1))
        g = (halves(m2), cross, halves(m2 * u2 + p), halves(m3 * u2), halves(ep * u2))
        for c in range(5):
            for x2 in range(2):
                frow = pl.multiple_of(128 * i + 16 * xp + 16 * x2, 16)
                for y8 in range(2):
                    at = 32 * x2 + 16 * y8
                    fbuf[c, 2 * yh + y8, pl.ds(frow, 16), zs] = f[c][at : at + 16]
                row = pl.multiple_of(64 * xp + 64 * x2 + 32 * yh, 32)
                gbuf[c, pl.ds(row, 32), zs] = g[c][32 * x2 : 32 * x2 + 32]

    def keep(right, left, c, rows, result):
        extra = result[256:]
        right[c, rows] = extra[0:8] + extra[16:24]
        left[c, rows] = extra[8:16] + extra[24:32]
        right[5 + c, rows] = extra[32:40]
        left[5 + c, rows] = extra[40:48]

    gs = (g0, g1)
    for i in range(5):
        if i < 4:
            for copy in copies[i]:
                copy.wait()

        def stage(c, carry, i=i):
            if i < 4:
                for j in range(PIECES):
                    piece(i, jnp.minimum(PIECES * c + j, 31), gs[i % 2])
            if i >= 1:
                xs = pl.ds(8 * (i - 1), 8)
                across = jnp.dot(ky[...], gs[(i - 1) % 2][c], preferred_element_type=F32)
                part[c, xs] = part[c, xs] - factor * across[:256].reshape(8, B, NZ)
                keep(yr, yl, c, xs, across)
            return carry

        lax.fori_loop(0, 5, stage, 0)

    def last(c, carry):
        for block in range(4):
            ys = pl.ds(8 * block, 8)
            slope = jnp.dot(kx[...], fbuf[c, block], preferred_element_type=F32)
            part[c, :, ys, :] = part[c, :, ys, :] - factor * slope[:256].reshape(B, 8, NZ)
            keep(xr, xl, c, ys, slope)
        return carry

    lax.fori_loop(0, 5, last, 0)


def xy_part(rho, mom, ene, after):
    return pl.pallas_call(
        xy_kernel,
        in_specs=[ANYWHERE] * 3 + [IN_VMEM] * 2 + [ANYWHERE],
        out_specs=[IN_VMEM] * 5,
        out_shape=[pltpu.VMEM((5, B, B, NZ), F32)] + [pltpu.VMEM((10, B, NZ), F32)] * 4,
        scratch_shapes=[
            pltpu.VMEM((5, 4, 512, NZ), BF16),
            pltpu.VMEM((5, 512, NZ), BF16),
            pltpu.VMEM((5, 512, NZ), BF16),
            pltpu.SemaphoreType.DMA((4, 3)),
        ],
        compiler_params=pltpu.CompilerParams(vmem_limit_bytes=24 << 20),
        name="xy_part",
    )(rho, mom, ene, jnp.asarray(block_matrix(False)), jnp.asarray(block_matrix(True)), after)


def z_kernel(first, start, rho, mom, ene, mz, after, part, state, h0, h1, sems):
    factor = STEP / SCALE
    copies = [state_copies(rho, mom, ene, state, sems, i, first) for i in range(2)]
    for group in copies:
        for copy in group:
            copy.start()

    def piece(i, k, hbuf):
        xp, yh, ys, zs = piece_slices(k)
        xs = pl.ds(8 * i + xp, 2)
        d, m1, m2, m3, e = (state[c, xs, ys, zs].reshape(4, 8, 128) for c in range(5))
        u1, u2, u3, p = state_parts(d, m1, m2, m3, e)
        h = [halves(v) for v in (m3, m1 * u3, m2 * u3, m3 * u3 + p, (e + p) * u3)]
        for c in range(5):
            for x2 in range(2):
                row = pl.multiple_of(64 * xp + 64 * x2 + 32 * yh, 32)
                hbuf[c, pl.ds(row, 32), zs] = h[c][32 * x2 : 32 * x2 + 32]

    hs = (h0, h1)
    for i in range(3):
        if i < 2:
            for copy in copies[i]:
                copy.wait()

        def stage(c, carry, i=i):
            if i < 2:
                for j in range(PIECES):
                    piece(i, jnp.minimum(PIECES * c + j, 31), hs[i % 2])
            if i >= 1:
                xs = pl.ds(8 * (first + i - 1), 8)
                along = jnp.dot(hs[(i - 1) % 2][c], mz[...], preferred_element_type=F32)
                along = along.reshape(32, 2, 8, NZ)
                along = along[:, 0] + along[:, 1]
                part[c, xs] = part[c, xs] - factor * along.reshape(8, B, NZ)
            return carry

        lax.fori_loop(0, 5, stage, 0)


def z_part(first, part, rho, mom, ene, after):
    return pl.pallas_call(
        functools.partial(z_kernel, first),
        in_specs=[IN_VMEM] + [ANYWHERE] * 3 + [IN_VMEM, ANYWHERE],
        out_specs=IN_VMEM,
        out_shape=pltpu.VMEM((5, B, B, NZ), F32),
        input_output_aliases={0: 0},
        scratch_shapes=[
            pltpu.VMEM((5, 16, B, NZ), F32),
            pltpu.VMEM((5, 512, NZ), BF16),
            pltpu.VMEM((5, 512, NZ), BF16),
            pltpu.SemaphoreType.DMA((2, 3)),
        ],
        compiler_params=pltpu.CompilerParams(vmem_limit_bytes=20 << 20),
        name="z_part",
    )(part, rho, mom, ene, jnp.asarray(z_matrix()), after)


def merge_kernel(kept, got, after, stay, leave):
    for h, source in enumerate((kept, got)):
        for a in range(4):
            to = pl.ds(32 * h + 8 * a, 8)
            stay[to, :] = source[pl.ds(16 * a, 8), :]
            leave[to, :] = source[pl.ds(16 * a + 8, 8), :]


def merge(kept, got, after):
    return pl.pallas_call(
        merge_kernel,
        in_specs=[IN_VMEM] * 2 + [ANYWHERE],
        out_specs=[IN_VMEM] * 2,
        out_shape=[pltpu.VMEM((64, 160), F32)] * 2,
        compiler_params=pltpu.CompilerParams(vmem_limit_bytes=1 << 20),
        name="merge_rows",
    )(kept, got, after)


def ghost_kernel(pick, kept, got, out):
    ghosts = jnp.dot(pick[:, 0:64], kept[...], precision=highest, preferred_element_type=F32)
    ghosts = ghosts + jnp.dot(pick[:, 64:128], got[...], precision=highest, preferred_element_type=F32)
    d, m1, m2, m3, e = (ghosts[:, 32 * c : 32 * c + 32] for c in range(5))
    u1, u2, u3, p = state_parts(d, m1, m2, m3, e)
    cell = lax.broadcasted_iota(jnp.int32, (128, 256), 0) % 8
    lane = lax.broadcasted_iota(jnp.int32, (128, 256), 1) // 32
    for c, h in enumerate((m3, m1 * u3, m2 * u3, m3 * u3 + p, (e + p) * u3)):
        out[c] = jnp.where(cell == lane, jnp.concatenate([h] * 8, axis=1), 0.0)


def ghost_flux(pick, kept, got):
    return pl.pallas_call(
        ghost_kernel,
        in_specs=[IN_VMEM] * 3,
        out_specs=IN_VMEM,
        out_shape=pltpu.VMEM((5, 128, 256), F32),
        compiler_params=pltpu.CompilerParams(vmem_limit_bytes=4 << 20),
        name="ghost_flux",
    )(pick, kept, got)


GROUP = 8


def finish_kernel(table, part, fl, fr, gl, gr, xr, xl, yr, yl, wy, ghost, mg, out, el, er, hl, hr, wu, slots, sems):
    inner = []
    place = lax.axis_index("gx"), lax.axis_index("gy")
    for at_end, own, got, kept in (
        (place[0] == 0, xl, fl, el),
        (place[0] == 15, xr, fr, er),
        (place[1] == 0, yl, gl, hl),
        (place[1] == 7, yr, gr, hr),
    ):
        inner.append(jnp.where(at_end, 0.0, 1.0).astype(F32))

        @pl.when(at_end)
        def _(own=own, kept=kept):
            for c in range(5):
                kept[c] = ROOT * own[c] + ((FIRST - TAIL * ROOT) / TAIL) * own[5 + c]

        @pl.when(jnp.logical_not(at_end))
        def _(got=got, kept=kept):
            for c in range(5):
                kept[c] = got[c]

    wu[0] = wy[0]
    wu[1] = wy[1] * inner[2]
    wu[2] = wy[2]
    wu[3] = wy[3] * inner[3]

    def group(step, carry):
        slot = step % 2
        xs = pl.ds(GROUP * step, GROUP)

        def copy_out(at):
            return pltpu.make_async_copy(slots.at[slot], out.at[:, pl.ds(GROUP * at, GROUP)], sems.at[slot])

        @pl.when(step >= 2)
        def _():
            copy_out(step - 2).wait()

        aligned = pl.ds(pl.multiple_of(GROUP * step, GROUP), GROUP)
        for c in range(5):
            lines = [ghost[c, pl.ds(pl.multiple_of(32 * k + GROUP * step, 8), 8), :] for k in range(4)]
            high, low = split(jnp.concatenate(lines, axis=0))
            zpart = lax.dot_general(
                jnp.concatenate([high, low, high], axis=0),
                mg[...],
                (((0,), (0,)), ((), ())),
                preferred_element_type=F32,
            )
            for q in range(4):
                zs = pl.ds(128 * q, 128)
                low, high = hl[c, aligned, zs], hr[c, aligned, zs]
                low_edge, high_edge = gl[5 + c, aligned, zs], gr[5 + c, aligned, zs]
                for k in range(GROUP):
                    x = GROUP * step + k
                    ql = table[0, x]
                    qr = table[2, x]
                    for t in range(4):
                        rows = pl.ds(8 * t, 8)
                        value = part[c, x, rows, zs] + ql * el[c, rows, zs] + qr * er[c, rows, zs]
                        value = value + wu[0, rows, :] * low[k : k + 1]
                        value = value + wu[2, rows, :] * high[k : k + 1]
                        if t == 0:
                            value = value + wu[1, rows, :] * low_edge[k : k + 1]
                        if t == 3:
                            value = value + wu[3, rows, :] * high_edge[k : k + 1]
                        if q == 0:
                            value = value + zpart[32 * k + 8 * t : 32 * k + 8 * t + 8, :128]
                        if q == 3:
                            value = value + zpart[32 * k + 8 * t : 32 * k + 8 * t + 8, 128:]
                        slots[slot, c, k, rows, zs] = value

        @pl.when(step == 0)
        def _():
            for c in range(5):
                slots[slot, c, 0] = slots[slot, c, 0] + (table[1, 0] * inner[0]) * fl[5 + c]

        @pl.when(step == B // GROUP - 1)
        def _():
            for c in range(5):
                slots[slot, c, GROUP - 1] = slots[slot, c, GROUP - 1] + (table[3, B - 1] * inner[1]) * fr[5 + c]

        copy_out(step).start()
        return carry

    lax.fori_loop(0, B // GROUP, group, 0)
    for slot in range(2):
        pltpu.make_async_copy(
            slots.at[slot], out.at[:, pl.ds(B - GROUP * (2 - slot), GROUP)], sems.at[slot]
        ).wait()


def finish(part, fl, fr, gl, gr, xr, xl, yr, yl, ghost):
    table = edge_weights()
    wy = np.broadcast_to(table[:, :, None], (4, B, 128))
    smem = pl.BlockSpec(memory_space=pltpu.SMEM)
    vmem = pl.BlockSpec(memory_space=pltpu.VMEM)
    return pl.pallas_call(
        finish_kernel,
        in_specs=[smem] + [vmem] * 12,
        out_specs=pl.BlockSpec(memory_space=pl.ANY),
        out_shape=jax.ShapeDtypeStruct((5, B, B, NZ), F32),
        scratch_shapes=[pltpu.VMEM((5, B, NZ), F32)] * 4
        + [pltpu.VMEM((4, B, 128), F32), pltpu.VMEM((2, 5, GROUP, B, NZ), F32), pltpu.SemaphoreType.DMA((2,))],
        compiler_params=pltpu.CompilerParams(vmem_limit_bytes=16 << 20),
        name="add_messages",
    )(
        jnp.asarray(table),
        part,
        fl,
        fr,
        gl,
        gr,
        xr,
        xl,
        yr,
        yl,
        jnp.asarray(wy),
        ghost,
        jnp.asarray(ghost_matrix()),
    )


def ring(array, axis, by):
    count = lax.axis_size(axis)
    return lax.ppermute(array, axis, [(i, (i + by) % count) for i in range(count)])


def rows_to_send(place_x, coarse, slot_rows, slot_times):
    devices = jnp.arange(16, dtype=jnp.int32)
    turn = (jnp.bitwise_xor(place_x, devices)[:, None] == devices[None, :]).astype(F32)
    both = jnp.concatenate([slot_rows, slot_times], axis=1).astype(F32)
    both = jnp.dot(turn, both, precision=highest)
    rows = both[:, :128] - (256 * place_x).astype(F32)
    weight = both[:, 128:] * 0.125
    mine = (rows >= 0.0) & (rows < 256.0)
    slots = jnp.arange(128)
    before = (slots[:, None] < slots[None, :]).astype(F32)
    rank = jnp.dot(mine.astype(F32), before, precision=highest)
    chosen = mine[:, None, :] & (rank[:, None, :] == jnp.arange(8, dtype=F32)[None, :, None])
    index = jnp.sum(jnp.where(chosen, rows[:, None, :], 0.0), axis=2)[:, :, None]
    late = jnp.sum(jnp.where(chosen, weight[:, None, :], 0.0), axis=2)[:, :, None]
    hit = index == jnp.arange(256, dtype=F32)[None, None, :]
    old = jnp.where(hit, 1.0 - late, 0.0)
    new = jnp.where(hit, late, 0.0)
    return jnp.einsum("dpr,rf->dpf", old, coarse[0], precision=highest) + jnp.einsum(
        "dpr,rf->dpf", new, coarse[1], precision=highest
    )


def trade(sent, bit):
    return lax.ppermute(sent, "gx", [(i, i ^ bit) for i in range(16)])


def slot_picks(place_x, slot_rows):
    own = lax.dynamic_index_in_dim(slot_rows, place_x, 0, keepdims=False)
    owner = own // 256
    slots = jnp.arange(128)
    same = (owner[:, None] == owner[None, :]) & (slots[None, :] < slots[:, None])
    rank = jnp.sum(same.astype(jnp.int32), axis=1)
    turn = jnp.bitwise_xor(owner, place_x)
    order = (turn // 4) * 4 + (turn % 2) * 2 + (turn // 2) % 2
    return (order[:, None] * 8 + rank[:, None] == slots[None, :]).astype(F32)


def local(density, momentum, energy, coarse_rows, ghost_rows, time_index):
    density, momentum, energy = (
        pltpu.with_memory_space_constraint(a, pltpu.HBM) for a in (density, momentum, energy)
    )
    place_x = lax.axis_index("gx")
    slot_rows = ghost_rows[0]
    rows = rows_to_send(place_x, coarse_rows[:, :, 0, :], slot_rows, time_index[0])
    pick = slot_picks(place_x, slot_rows)
    rows = rows.reshape(4, 2, 2, 8, 160)
    kept, sent = rows[:, 0].reshape(64, 160), rows[:, 1].reshape(64, 160)
    kept, sent, pick = lax.optimization_barrier((kept, sent, pick))
    got = trade(sent, 2)
    kept, sent = merge(kept, got, pick)
    got = trade(sent, 1)
    part, xr, xl, yr, yl = xy_part(density, momentum, energy, sent)
    kept, sent = merge(kept, got, xr)
    xr, xl, yr, yl, sent = lax.optimization_barrier((xr, xl, yr, yl, sent))
    fl = ring(xr, "gx", 1)
    fr = ring(xl, "gx", -1)
    gl = ring(yr, "gy", 1)
    gr = ring(yl, "gy", -1)
    got = trade(sent, 4)
    part = z_part(0, part, density, momentum, energy, sent)
    kept, sent = merge(kept, got, part)
    got = trade(sent, 8)
    part = z_part(2, part, density, momentum, energy, sent)
    ghost = ghost_flux(pick, kept, got)
    return finish(part, fl, fr, gl, gr, xr, xl, yr, yl, ghost)


def solution(mesh):
    return jax.shard_map(
        local,
        mesh=mesh,
        in_specs=(
            P("gx", "gy", None),
            P(None, "gx", "gy", None),
            P("gx", "gy", None),
            P(None, "gx", "gy", None),
            P("gy", None, None),
            P("gy", None, None),
        ),
        out_specs=P(None, "gx", "gy", None),
        check_vma=False,
    )
```

time: 314 us -> 73.7 us (0.23)
  other arithmetic: 109 us -> 1.87 us
  matrix products: 97.5 us -> 3.55 us
  local copies, waits for them, and re-layouts: 58.7 us -> 2.04 us
  Pallas kernels: 0 us -> 42.5 us
  starting transfers between devices: 33.7 us -> 17.7 us
  between operations: 5.17 us -> 0.2 us
    dot_general x3 -> x4, matrix products: 97.5 us -> 3.55 us  [the longest x1 1.26 us: rows_to_send(): jnp.einsum('dpr,rf->dpf', new, coarse[1], precision=highest)]
    pallas_call x0 -> x8, Pallas kernels: none -> 42.5 us  [the longest x1 19 us: xy_part(): pl.pallas_call(xy_kernel, in_specs=[ANYWHERE] * 3 + [IN_VMEM] * 2 + [ANYW...]
    select_n x11 -> x1, other arithmetic: 36.4 us -> 0.76 us  [slot_picks(): owner = own // 256]
    unnamed x10 -> x0, other arithmetic: 20.4 us -> none
    concatenate x2 -> x0, other arithmetic: 20.1 us -> none  [the longest x1 10.6 us: local(): fields = jnp.concatenate([density[None], momentum, energy[None]], axis=0)]
    add x5 -> x1, other arithmetic: 20.7 us -> 0.73 us  [slot_picks(): return (order[:, None] * 8 + rank[:, None] == slots[None, :]).astype(F32)]
    dot_general x1 -> x0, local copies, waits for them, and re-layouts: 14.3 us -> none  [local(): jnp.einsum('ij,fjyz->fiyz', block_inverse, right_x, precision=highest)]
    slice x7 -> x1, local copies, waits for them, and re-layouts: 12.4 us -> 0.01 us  [local(): kept, sent = (rows[:, 0].reshape(64, 160), rows[:, 1].reshape(64, 160))]
  transfers between devices with their start and end apart: 9 -> 8, of which waited for: 1 -> 2; matrix products, arithmetic and copies ran while one was open for 54% -> 0% of each run, Pallas kernels for 0% -> 49%
where the time goes in v1:
time: 73.7 us; the launch traced here: 72.3 us
  Pallas kernels  42.5 us (58%)
  starting transfers between devices  17.7 us (24%)
  waiting for transfers between devices  4.47 us (6%)
  matrix products  3.55 us (5%)
  local copies, waits for them, and re-layouts  2.04 us (3%)
  other arithmetic  1.87 us (3%)
    pallas_call x1, Pallas kernels, xy_part(): pl.pallas_call(xy_kernel, in_specs=[ANYWHERE] * 3 + [IN_VMEM] * 2 + [ANYW...  19 us
    pallas_call x2, Pallas kernels, z_part(): pl.pallas_call(functools.partial(z_kernel, first), in_specs=[IN_VMEM] + [...  15.6 us
    ppermute x4, starting transfers between devices, ring(): lax.ppermute(array, axis, [(i, (i + by) % count) for i in range(count)])  9.01 us
    ppermute x4, starting transfers between devices, trade(): return lax.ppermute(sent, 'gx', [(i, i ^ bit) for i in range(16)])  8.67 us
    pallas_call x1, Pallas kernels, finish(): pl.pallas_call(finish_kernel, in_specs=[smem] + [vmem] * 12, out_specs=pl...  6.99 us
    ppermute x4, waiting for transfers between devices, trade(): return lax.ppermute(sent, 'gx', [(i, i ^ bit) for i in range(16)])  4.46 us
    unnamed x10, local copies, waits for them, and re-layouts  1.95 us
  transfers between devices with their start and end apart: 8, of which 2 were waited for; matrix products, arithmetic and copies ran while one was open for 0% of the time, Pallas kernels for 49%

profile of v1, /device:TPU:1, one launch (start us, length us, event | category | flops | bytes accessed | tf_op | source)
XLA Modules:
  0.0 72.3 jit_solution(15313874954926599508)
XLA Ops:
  0.0 0.0 copy-start
  0.0 0.8 %and_select_fusion.4 = s32[128]{0:T(128)S(1)} fusion(s32[1,16,128]{2,1,0:T(8,128)} %param.17, s32[]{:T(128)S(6)} %select_n.71), kind=kLoop, calls=%fused_computation.42 | loop fusion | flops 1920 | bytes 1028 | tf_op jit(solution)/shard_map/jit(floor_divide)/jit(_where)/select_n | solution.py:464
  0.8 0.2 convert_reduce_fusion
  0.9 0.7 %multiply_add_fusion = s32[128]{0:T(128)S(1)} fusion(s32[128]{0:T(128)S(1)} %convert_reduce_fusion, s32[]{:T(128)S(6)} %axis_index.15, s32[1,16,128]{2,1,0:T(8,128)} %param.17, s32[]{:T(128)S(6)} %select_n.71), kind=kLoop, calls=%fused_computation.56 | loop fusion | flops 7936 | bytes 1544 | tf_op jit(solution)/shard_map/add | solution.py:470
  1.7 0.9 %fusion.17 = f32[16,256]{1,0:T(8,128)S(1)} fusion(s32[16,128]{1,0:T(8,128)} %bitcast.34, s32[16,128]{1,0:T(8,128)} %bitcast.33, s32[16]{0:T(128)S(1)} %iota_xor_fusion), kind=kOutput, calls=%fused_computation.27 | convolution fusion | flops 794880 | bytes 32832 | tf_op jit(solution)/shard_map/dot_general | solution.py:440
  2.6 0.1 fusion.16
  2.7 0.1 select_reduce_fusion.1
  2.9 0.1 fusion.15.after.pick
  3.0 1.3 %fusion.1 = f32[16,8,160]{2,1,0:T(8,128)S(1)} fusion(f32[2,256,1,160]{1,3,2,0:T(8,128)} %param.16, f32[16,8]{1,0:T(8,128)S(1)} %broadcast_subtract_fusion, f32[16,8]{1,0:T(8,128)S(1)} %get-tuple-element.43), kind=kOutput, calls=%fused_computation.2 | convolution fusion | flops 62980096 | bytes 246784 | tf_op jit(solution)/shard_map/dpr,rf->dpf/dot_general | solution.py:453
  4.2 1.3 %convolution_add_fusion = f32[16,8,160]{2,1,0:T(8,128)S(1)} fusion(f32[16,8,160]{2,1,0:T(8,128)S(1)} %fusion.1, f32[2,256,1,160]{1,3,2,0:T(8,128)} %param.16, f32[16,8]{1,0:T(8,128)S(1)} %get-tuple-element.44, f32[16,8]{1,0:T(8,128)S(1)} %get-tuple-element.43), kind=kOutput, calls=%fused_computation | convolution fusion | flops 63000576 | bytes 328704 | tf_op jit(solution)/shard_map/dpr,rf->dpf/dot_general | solution.py:453
  5.5 3.8 %collective-permute-start = (f32[64,160]{1,0:T(8,128)S(1)}, f32[64,160]{1,0:T(8,128)S(1)}, u32[]{:S(2)}, u32[]{:S(2)}) collective-permute-start(f32[64,160]{1,0:T(8,128)S(1)} %bitcast.32), channel_id=1, source_target_pairs={{0,16},{8,24},{16,0},{24,8},{32,48},{40,56},{48,32},{56,40},{64,80... | collective-permute-start | bytes 122888 | tf_op jit(solution)/shard_map/ppermute | solution.py:459
  9.3 1.7 %collective-permute-done.got = f32[64,160]{1,0:T(8,128)S(1)} collective-permute-done((f32[64,160]{1,0:T(8,128)S(1)}, f32[64,160]{1,0:T(8,128)S(1)}, u32[]{:S(2)}, u32[]{:S(2)}) %collective-permute-start) | collective-permute-done | bytes 40992 | tf_op jit(solution)/shard_map/ppermute | solution.py:459
  11.0 1.4 %collective-permute-start.1 = (f32[64,160]{1,0:T(8,128)S(1)}, f32[64,160]{1,0:T(8,128)S(1)}, u32[]{:S(2)}, u32[]{:S(2)}) collective-permute-start(f32[64,160]{1,0:T(8,128)S(1)} %get-tuple-element.27.after), channel_id=1, source_target_pairs={{0,8},{8,0},{16,24},{24,16},{32,40},{40,32},{48,56},{56,48},{64,72... | collective-permute-start | bytes 122888 | tf_op jit(solution)/shard_map/ppermute | solution.py:459
  12.4 0.0 copy-start.1
  12.4 1.0 %copy-done.1 = bf16[304,512]{1,0:T(8,128)(2,1)S(1)} copy-done((bf16[304,512]{1,0:T(8,128)(2,1)S(1)}, bf16[304,512]{1,0:T(8,128)(2,1)}, u32[]{:S(2)}) %copy-start.1) | copy-done | bytes 311320
  13.4 0.0 copy-start.2
  13.4 1.0 %copy-done.2 = bf16[304,512]{1,0:T(8,128)(2,1)S(1)} copy-done((bf16[304,512]{1,0:T(8,128)(2,1)S(1)}, bf16[304,512]{1,0:T(8,128)(2,1)}, u32[]{:S(2)}) %copy-start.2) | copy-done | bytes 311320
  14.4 19.0 %xy_part.1 = (f32[5,32,32,512]{3,2,1,0:T(8,128)S(1)}, f32[10,32,512]{2,1,0:T(8,128)S(1)}, f32[10,32,512]{2,1,0:T(8,128)S(1)}, f32[10,32,512]{2,1,0:T(8,128)S(1)}, f32[10,32,512]{2,1,0:T(8,128)S(1)}) custom-call(f32[32,32,512]{2,1,0:T(8,128)} %rho.5, f32[3,32,32,512]{3,2,1,0:T(8,128)} %mom.5, f32[32,32,512]{2,1,0:T(8,128)} %ene.5, ...), custom_call_target="tpu_custom_call" | custom-call | tf_op jit(solution)/shard_map/xy_part/pallas_call | solution.py:193
  33.3 0.0 collective-permute-done.1.got
  33.4 0.2 collective-permute-start.3
  33.6 5.3 %collective-permute-start.4 = (f32[10,32,512]{2,1,0:T(8,128)S(1)}, f32[10,32,512]{2,1,0:T(8,128)S(1)}, u32[]{:S(2)}, u32[]{:S(2)}) collective-permute-start(f32[10,32,512]{2,1,0:T(8,128)S(1)} %get-tuple-element.39.xl), channel_id=1, source_target_pairs={{0,120},{8,0},{16,8},{24,16},{32,24},{40,32},{48,40},{56,48},{64,5... | collective-permute-start | bytes 1966088 | tf_op jit(solution)/shard_map/ppermute | solution.py:433
  38.9 3.5 %collective-permute-start.5 = (f32[10,32,512]{2,1,0:T(8,128)S(1)}, f32[10,32,512]{2,1,0:T(8,128)S(1)}, u32[]{:S(2)}, u32[]{:S(2)}) collective-permute-start(f32[10,32,512]{2,1,0:T(8,128)S(1)} %get-tuple-element.40.yr), channel_id=1, source_target_pairs={{0,1},{1,2},{2,3},{3,4},{4,5},{5,6},{6,7},{7,0},{8,9},{9,10},{10,1... | collective-permute-start | bytes 1966088 | tf_op jit(solution)/shard_map/ppermute | solution.py:433
  42.4 0.0 collective-permute-start.6
  42.4 0.0 collective-permute-start.2
  42.4 0.0 copy-done
  42.4 7.8 %z_part.2.after.start = f32[5,32,32,512]{3,2,1,0:T(8,128)S(1)} custom-call(f32[5,32,32,512]{3,2,1,0:T(8,128)S(1)} %get-tuple-element.28.start, f32[32,32,512]{2,1,0:T(8,128)} %rho.5, f32[3,32,32,512]{3,2,1,0:T(8,128)} %mom.5, f32[32,32,512]{2,1,0:T(8,128)} %ene.5, bf16[512,512]{1,0:T(8,128)(2,1)S(1)} %copy-done, ...), custom_call_target="tpu_custom_call", output_to_operand_aliasing={{}: (0, {})} | custom-call | tf_op jit(solution)/shard_map/z_part/pallas_call | solution.py:249
  50.3 2.8 %collective-permute-done.2.got = f32[64,160]{1,0:T(8,128)S(1)} collective-permute-done((f32[64,160]{1,0:T(8,128)S(1)}, f32[64,160]{1,0:T(8,128)S(1)}, u32[]{:S(2)}, u32[]{:S(2)}) %collective-permute-start.2) | collective-permute-done | bytes 40992 | tf_op jit(solution)/shard_map/ppermute | solution.py:459
  53.1 0.0 copy-start.4
  53.1 0.0 copy-start.3
  53.1 3.4 %collective-permute-start.7 = (f32[64,160]{1,0:T(8,128)S(1)}, f32[64,160]{1,0:T(8,128)S(1)}, u32[]{:S(2)}, u32[]{:S(2)}) collective-permute-start(f32[64,160]{1,0:T(8,128)S(1)} %get-tuple-element.37.after), channel_id=1, source_target_pairs={{0,64},{8,72},{16,80},{24,88},{32,96},{40,104},{48,112},{56,120},{... | collective-permute-start | bytes 122888 | tf_op jit(solution)/shard_map/ppermute | solution.py:459
  56.5 7.8 %z_part.3.part = f32[5,32,32,512]{3,2,1,0:T(8,128)S(1)} custom-call(f32[5,32,32,512]{3,2,1,0:T(8,128)S(1)} %z_part.2.after.start, f32[32,32,512]{2,1,0:T(8,128)} %rho.5, f32[3,32,32,512]{3,2,1,0:T(8,128)} %mom.5, f32[32,32,512]{2,1,0:T(8,128)} %ene.5, bf16[512,512]{1,0:T(8,128)(2,1)S(1)} %copy-done, ...), custom_call_target="tpu_custom_call", output_to_operand_aliasing={{}: (0, {})} | custom-call | tf_op jit(solution)/shard_map/z_part/pallas_call | solution.py:249
  64.3 0.0 collective-permute-done.7.got
  64.3 0.9 %ghost_flux.1.ghost = f32[5,128,256]{2,1,0:T(8,128)S(1)} custom-call(f32[128,128]{1,0:T(8,128)S(1)} %fusion.15.after.pick, f32[64,160]{1,0:T(8,128)S(1)} %get-tuple-element.42.kept, f32[64,160]{1,0:T(8,128)S(1)} %collective-permute-done.7.got), custom_call_target="tpu_custom_call" | custom-call | tf_op jit(solution)/shard_map/ghost_flux/pallas_call | solution.py:297
  65.2 0.0 collective-permute-done.3.fl
  65.2 0.0 collective-permute-done.4.fr
  65.2 0.0 collective-permute-done.5.gl
  65.2 0.0 collective-permute-done.6.gr
  65.2 0.0 copy-done.4
  65.2 0.1 jit_solution_.3.wy
  65.3 0.0 copy-done.3
  65.3 7.0 %add_messages.1 = f32[5,32,32,512]{3,2,1,0:T(8,128)} custom-call(f32[4,32]{1,0:T(4,128)S(1)} %copy-done.4, f32[5,32,32,512]{3,2,1,0:T(8,128)S(1)} %z_part.3.part, f32[10,32,512]{2,1,0:T(8,128)S(1)} %collective-permute-done.3.fl, f32[10,32,512]{2,1,0:T(8,128)S(1)} %collective-permute-done.4.fr, f32[10,32,512]{2,1,0:T(8,128)S(1)} %collective-permute-done.5.gl, ...), custom_call_target="tpu_custom_call" | custom-call | tf_op jit(solution)/shard_map/add_messages/pallas_call | solution.py:405
  (8 shorter events, 0.1 us)
Async XLA Ops:
  0.0 42.4 %copy-start = (bf16[512,512]{1,0:T(8,128)(2,1)S(1)}, bf16[512,512]{1,0:T(8,128)(2,1)}, u32[]{:S(2)}) copy-start(bf16[512,512]{1,0:T(8,128)(2,1)} %constant.91.clone.mz) | copy-start | bytes 1572868
  5.5 5.5 %collective-permute-start = (f32[64,160]{1,0:T(8,128)S(1)}, f32[64,160]{1,0:T(8,128)S(1)}, u32[]{:S(2)}, u32[]{:S(2)}) collective-permute-start(f32[64,160]{1,0:T(8,128)S(1)} %bitcast.32), channel_id=1, source_target_pairs={{0,16},{8,24},{16,0},{24,8},{32,48},{40,56},{48,32},{56,40},{64,80... | collective-permute-start | bytes 122888 | tf_op jit(solution)/shard_map/ppermute | solution.py:459
  11.0 22.4 %collective-permute-start.1 = (f32[64,160]{1,0:T(8,128)S(1)}, f32[64,160]{1,0:T(8,128)S(1)}, u32[]{:S(2)}, u32[]{:S(2)}) collective-permute-start(f32[64,160]{1,0:T(8,128)S(1)} %get-tuple-element.27.after), channel_id=1, source_target_pairs={{0,8},{8,0},{16,24},{24,16},{32,40},{40,32},{48,56},{56,48},{64,72... | collective-permute-start | bytes 122888 | tf_op jit(solution)/shard_map/ppermute | solution.py:459
  12.4 1.0 %copy-start.1 = (bf16[304,512]{1,0:T(8,128)(2,1)S(1)}, bf16[304,512]{1,0:T(8,128)(2,1)}, u32[]{:S(2)}) copy-start(bf16[304,512]{1,0:T(8,128)(2,1)} %constant.90.clone.ky) | copy-start | bytes 933892
  13.4 1.0 %copy-start.2 = (bf16[304,512]{1,0:T(8,128)(2,1)S(1)}, bf16[304,512]{1,0:T(8,128)(2,1)}, u32[]{:S(2)}) copy-start(bf16[304,512]{1,0:T(8,128)(2,1)} %constant.89.clone.kx) | copy-start | bytes 933892
  33.4 31.8 %collective-permute-start.3 = (f32[10,32,512]{2,1,0:T(8,128)S(1)}, f32[10,32,512]{2,1,0:T(8,128)S(1)}, u32[]{:S(2)}, u32[]{:S(2)}) collective-permute-start(f32[10,32,512]{2,1,0:T(8,128)S(1)} %get-tuple-element.38.after.xr), channel_id=1, source_target_pairs={{0,8},{8,16},{16,24},{24,32},{32,40},{40,48},{48,56},{56,64},{64,7... | collective-permute-start | bytes 1966088 | tf_op jit(solution)/shard_map/ppermute | solution.py:433
  33.6 31.6 %collective-permute-start.4 = (f32[10,32,512]{2,1,0:T(8,128)S(1)}, f32[10,32,512]{2,1,0:T(8,128)S(1)}, u32[]{:S(2)}, u32[]{:S(2)}) collective-permute-start(f32[10,32,512]{2,1,0:T(8,128)S(1)} %get-tuple-element.39.xl), channel_id=1, source_target_pairs={{0,120},{8,0},{16,8},{24,16},{32,24},{40,32},{48,40},{56,48},{64,5... | collective-permute-start | bytes 1966088 | tf_op jit(solution)/shard_map/ppermute | solution.py:433
  38.9 26.3 %collective-permute-start.5 = (f32[10,32,512]{2,1,0:T(8,128)S(1)}, f32[10,32,512]{2,1,0:T(8,128)S(1)}, u32[]{:S(2)}, u32[]{:S(2)}) collective-permute-start(f32[10,32,512]{2,1,0:T(8,128)S(1)} %get-tuple-element.40.yr), channel_id=1, source_target_pairs={{0,1},{1,2},{2,3},{3,4},{4,5},{5,6},{6,7},{7,0},{8,9},{9,10},{10,1... | collective-permute-start | bytes 1966088 | tf_op jit(solution)/shard_map/ppermute | solution.py:433
  42.4 22.8 %collective-permute-start.6 = (f32[10,32,512]{2,1,0:T(8,128)S(1)}, f32[10,32,512]{2,1,0:T(8,128)S(1)}, u32[]{:S(2)}, u32[]{:S(2)}) collective-permute-start(f32[10,32,512]{2,1,0:T(8,128)S(1)} %get-tuple-element.41.yl), channel_id=1, source_target_pairs={{0,7},{1,0},{2,1},{3,2},{4,3},{5,4},{6,5},{7,6},{8,15},{9,8},{10,9... | collective-permute-start | bytes 1966088 | tf_op jit(solution)/shard_map/ppermute | solution.py:433
  42.4 10.7 %collective-permute-start.2 = (f32[64,160]{1,0:T(8,128)S(1)}, f32[64,160]{1,0:T(8,128)S(1)}, u32[]{:S(2)}, u32[]{:S(2)}) collective-permute-start(f32[64,160]{1,0:T(8,128)S(1)} %get-tuple-element.35.after), channel_id=1, source_target_pairs={{0,32},{8,40},{16,48},{24,56},{32,0},{40,8},{48,16},{56,24},{64,96... | collective-permute-start | bytes 122888 | tf_op jit(solution)/shard_map/ppermute | solution.py:459
  53.1 12.2 %copy-start.4 = (f32[4,32]{1,0:T(4,128)S(1)}, f32[4,32]{1,0:T(4,128)}, u32[]{:S(2)}) copy-start(f32[4,32]{1,0:T(4,128)} %constant.92.clone.table) | copy-start | bytes 1540
  53.1 12.2 %copy-start.3 = (bf16[96,256]{1,0:T(8,128)(2,1)S(1)}, bf16[96,256]{1,0:T(8,128)(2,1)}, u32[]{:S(2)}) copy-start(bf16[96,256]{1,0:T(8,128)(2,1)} %constant.94.clone.mg) | copy-start | bytes 147460
  53.1 11.2 %collective-permute-start.7 = (f32[64,160]{1,0:T(8,128)S(1)}, f32[64,160]{1,0:T(8,128)S(1)}, u32[]{:S(2)}, u32[]{:S(2)}) collective-permute-start(f32[64,160]{1,0:T(8,128)S(1)} %get-tuple-element.37.after), channel_id=1, source_target_pairs={{0,64},{8,72},{16,80},{24,88},{32,96},{40,104},{48,112},{56,120},{... | collective-permute-start | bytes 122888 | tf_op jit(solution)/shard_map/ppermute | solution.py:459

commit v2 on v1

--- a/solution.py
+++ b/solution.py
@@ -109,6 +109,10 @@
 IN_VMEM = pl.BlockSpec(memory_space=pltpu.VMEM)
 
 
+def in_hbm(array):
+    return pltpu.with_memory_space_constraint(array, pltpu.HBM)
+
+
 def piece_slices(k):
     xs = 2 * (k // 8)
     yh = (k // 4) % 2
@@ -117,27 +121,41 @@
     return xs, yh, ys, zs
 
 
-def state_copies(rho, mom, ene, state, sems, i, first=0):
-    xs = pl.ds(8 * (first + i), 8)
-    to = pl.ds(8 * i, 8)
-    return (
-        pltpu.make_async_copy(rho.at[xs], state.at[0, to], sems.at[i, 0]),
-        pltpu.make_async_copy(mom.at[:, xs], state.at[1:4, to], sems.at[i, 1]),
-        pltpu.make_async_copy(ene.at[xs], state.at[4, to], sems.at[i, 2]),
-    )
-
-
-def xy_kernel(rho, mom, ene, kx, ky, after, part, xr, xl, yr, yl, fbuf, g0, g1, sems):
+def load_pieces(state, xs, ys, zs):
+    return tuple(state[c, xs, ys, zs].reshape(4, 8, 128) for c in range(5))
+
+
+def keep(right, left, c, rows, result):
+    extra = result[256:]
+    right[c, rows] = extra[0:8] + extra[16:24]
+    left[c, rows] = extra[8:16] + extra[24:32]
+    right[5 + c, rows] = extra[32:40]
+    left[5 + c, rows] = extra[40:48]
+
+
+def y_kernel(first, *refs):
+    rho, mom, ene, ky_in, after = refs[:5]
+    state, part, fbuf, yr, yl, g0, g1, ky, sems = refs[-9:]
     factor = STEP / SCALE
-    copies = [state_copies(rho, mom, ene, part, sems, i) for i in range(4)]
-    for group in copies:
-        for copy in group:
+    copies = []
+    for i in range(2):
+        xs = pl.ds(8 * (first + i), 8)
+        copies.append(
+            (
+                pltpu.make_async_copy(rho.at[xs], state.at[0, xs], sems.at[i, 0]),
+                pltpu.make_async_copy(mom.at[:, xs], state.at[1:4, xs], sems.at[i, 1]),
+                pltpu.make_async_copy(ene.at[xs], state.at[4, xs], sems.at[i, 2]),
+            )
+        )
+        for copy in copies[-1]:
             copy.start()
+
+    matrix = pltpu.make_async_copy(ky_in, ky, sems.at[2, 0])
+    matrix.start()
 
     def piece(i, k, gbuf):
         xp, yh, ys, zs = piece_slices(k)
-        xs = pl.ds(8 * i + xp, 2)
-        d, m1, m2, m3, e = (part[c, xs, ys, zs].reshape(4, 8, 128) for c in range(5))
+        d, m1, m2, m3, e = load_pieces(state, pl.ds(8 * (first + i) + xp, 2), ys, zs)
         u1, u2, u3, p = state_parts(d, m1, m2, m3, e)
         ep = e + p
         cross = halves(m1 * u2)
@@ -145,40 +163,63 @@
         g = (halves(m2), cross, halves(m2 * u2 + p), halves(m3 * u2), halves(ep * u2))
         for c in range(5):
             for x2 in range(2):
-                frow = pl.multiple_of(128 * i + 16 * xp + 16 * x2, 16)
+                frow = pl.multiple_of(128 * (first + i) + 16 * xp + 16 * x2, 16)
                 for y8 in range(2):
                     at = 32 * x2 + 16 * y8
                     fbuf[c, 2 * yh + y8, pl.ds(frow, 16), zs] = f[c][at : at + 16]
                 row = pl.multiple_of(64 * xp + 64 * x2 + 32 * yh, 32)
                 gbuf[c, pl.ds(row, 32), zs] = g[c][32 * x2 : 32 * x2 + 32]
 
-    def keep(right, left, c, rows, result):
-        extra = result[256:]
-        right[c, rows] = extra[0:8] + extra[16:24]
-        left[c, rows] = extra[8:16] + extra[24:32]
-        right[5 + c, rows] = extra[32:40]
-        left[5 + c, rows] = extra[40:48]
-
     gs = (g0, g1)
-    for i in range(5):
-        if i < 4:
+    for i in range(3):
+        if i < 2:
             for copy in copies[i]:
                 copy.wait()
+        if i == 1:
+            matrix.wait()
 
         def stage(c, carry, i=i):
-            if i < 4:
+            if i < 2:
                 for j in range(PIECES):
                     piece(i, jnp.minimum(PIECES * c + j, 31), gs[i % 2])
             if i >= 1:
-                xs = pl.ds(8 * (i - 1), 8)
+                xs = pl.ds(8 * (first + i - 1), 8)
                 across = jnp.dot(ky[...], gs[(i - 1) % 2][c], preferred_element_type=F32)
-                part[c, xs] = part[c, xs] - factor * across[:256].reshape(8, B, NZ)
+                part[c, xs] = state[c, xs] - factor * across[:256].reshape(8, B, NZ)
                 keep(yr, yl, c, xs, across)
             return carry
 
         lax.fori_loop(0, 5, stage, 0)
 
-    def last(c, carry):
+
+def y_part(first, rho, mom, ene, after, begun=()):
+    return pl.pallas_call(
+        functools.partial(y_kernel, first),
+        in_specs=[ANYWHERE] * 5 + [IN_VMEM] * len(begun),
+        out_specs=[IN_VMEM] * 5,
+        out_shape=[
+            pltpu.VMEM((5, B, B, NZ), F32),
+            pltpu.VMEM((5, B, B, NZ), F32),
+            pltpu.VMEM((5, 4, 512, NZ), BF16),
+            pltpu.VMEM((10, B, NZ), F32),
+            pltpu.VMEM((10, B, NZ), F32),
+        ],
+        input_output_aliases={5 + i: i for i in range(len(begun))},
+        scratch_shapes=[
+            pltpu.VMEM((5, 512, NZ), BF16),
+            pltpu.VMEM((5, 512, NZ), BF16),
+            pltpu.VMEM((304, 512), BF16),
+            pltpu.SemaphoreType.DMA((3, 3)),
+        ],
+        compiler_params=pltpu.CompilerParams(vmem_limit_bytes=12 << 20),
+        name="y_part",
+    )(rho, mom, ene, in_hbm(jnp.asarray(block_matrix(True))), after, *begun)
+
+
+def x_kernel(start, fbuf, kx, after, part, xr, xl):
+    factor = STEP / SCALE
+
+    def component(c, carry):
         for block in range(4):
             ys = pl.ds(8 * block, 8)
             slope = jnp.dot(kx[...], fbuf[c, block], preferred_element_type=F32)
@@ -186,37 +227,27 @@
             keep(xr, xl, c, ys, slope)
         return carry
 
-    lax.fori_loop(0, 5, last, 0)
-
-
-def xy_part(rho, mom, ene, after):
-    return pl.pallas_call(
-        xy_kernel,
-        in_specs=[ANYWHERE] * 3 + [IN_VMEM] * 2 + [ANYWHERE],
-        out_specs=[IN_VMEM] * 5,
-        out_shape=[pltpu.VMEM((5, B, B, NZ), F32)] + [pltpu.VMEM((10, B, NZ), F32)] * 4,
-        scratch_shapes=[
-            pltpu.VMEM((5, 4, 512, NZ), BF16),
-            pltpu.VMEM((5, 512, NZ), BF16),
-            pltpu.VMEM((5, 512, NZ), BF16),
-            pltpu.SemaphoreType.DMA((4, 3)),
-        ],
-        compiler_params=pltpu.CompilerParams(vmem_limit_bytes=24 << 20),
-        name="xy_part",
-    )(rho, mom, ene, jnp.asarray(block_matrix(False)), jnp.asarray(block_matrix(True)), after)
-
-
-def z_kernel(first, start, rho, mom, ene, mz, after, part, state, h0, h1, sems):
+    lax.fori_loop(0, 5, component, 0)
+
+
+def x_part(part, fbuf, after):
+    return pl.pallas_call(
+        x_kernel,
+        in_specs=[IN_VMEM] * 3 + [ANYWHERE],
+        out_specs=[IN_VMEM] * 3,
+        out_shape=[pltpu.VMEM((5, B, B, NZ), F32)] + [pltpu.VMEM((10, B, NZ), F32)] * 2,
+        input_output_aliases={0: 0},
+        compiler_params=pltpu.CompilerParams(vmem_limit_bytes=6 << 20),
+        name="x_part",
+    )(part, fbuf, jnp.asarray(block_matrix(False)), after)
+
+
+def z_kernel(start, state, mz, after, part, h0, h1):
     factor = STEP / SCALE
-    copies = [state_copies(rho, mom, ene, state, sems, i, first) for i in range(2)]
-    for group in copies:
-        for copy in group:
-            copy.start()
 
     def piece(i, k, hbuf):
         xp, yh, ys, zs = piece_slices(k)
-        xs = pl.ds(8 * i + xp, 2)
-        d, m1, m2, m3, e = (state[c, xs, ys, zs].reshape(4, 8, 128) for c in range(5))
+        d, m1, m2, m3, e = load_pieces(state, pl.ds(8 * i + xp, 2), ys, zs)
         u1, u2, u3, p = state_parts(d, m1, m2, m3, e)
         h = [halves(v) for v in (m3, m1 * u3, m2 * u3, m3 * u3 + p, (e + p) * u3)]
         for c in range(5):
@@ -225,42 +256,37 @@
                 hbuf[c, pl.ds(row, 32), zs] = h[c][32 * x2 : 32 * x2 + 32]
 
     hs = (h0, h1)
-    for i in range(3):
-        if i < 2:
-            for copy in copies[i]:
-                copy.wait()
+    for i in range(5):
 
         def stage(c, carry, i=i):
-            if i < 2:
-                for j in range(PIECES):
+            along = []
+            for j in range(PIECES):
+                if i < 4:
                     piece(i, jnp.minimum(PIECES * c + j, 31), hs[i % 2])
-            if i >= 1:
-                xs = pl.ds(8 * (first + i - 1), 8)
-                along = jnp.dot(hs[(i - 1) % 2][c], mz[...], preferred_element_type=F32)
-                along = along.reshape(32, 2, 8, NZ)
-                along = along[:, 0] + along[:, 1]
-                part[c, xs] = part[c, xs] - factor * along.reshape(8, B, NZ)
+                if i >= 1 and j in (1, 3):
+                    rows = pl.ds(256 * len(along), 256)
+                    both = jnp.dot(hs[(i - 1) % 2][c, rows], mz[...], preferred_element_type=F32)
+                    both = both.reshape(16, 2, 8, NZ)
+                    along.append(both[:, 0] + both[:, 1])
+            for half, value in enumerate(along):
+                xs = pl.ds(8 * (i - 1) + 4 * half, 4)
+                part[c, xs] = part[c, xs] - factor * value.reshape(4, B, NZ)
             return carry
 
         lax.fori_loop(0, 5, stage, 0)
 
 
-def z_part(first, part, rho, mom, ene, after):
-    return pl.pallas_call(
-        functools.partial(z_kernel, first),
-        in_specs=[IN_VMEM] + [ANYWHERE] * 3 + [IN_VMEM, ANYWHERE],
+def z_part(part, state, after):
+    return pl.pallas_call(
+        z_kernel,
+        in_specs=[IN_VMEM] * 3 + [ANYWHERE],
         out_specs=IN_VMEM,
         out_shape=pltpu.VMEM((5, B, B, NZ), F32),
         input_output_aliases={0: 0},
-        scratch_shapes=[
-            pltpu.VMEM((5, 16, B, NZ), F32),
-            pltpu.VMEM((5, 512, NZ), BF16),
-            pltpu.VMEM((5, 512, NZ), BF16),
-            pltpu.SemaphoreType.DMA((2, 3)),
-        ],
-        compiler_params=pltpu.CompilerParams(vmem_limit_bytes=20 << 20),
+        scratch_shapes=[pltpu.VMEM((5, 512, NZ), BF16), pltpu.VMEM((5, 512, NZ), BF16)],
+        compiler_params=pltpu.CompilerParams(vmem_limit_bytes=12 << 20),
         name="z_part",
-    )(part, rho, mom, ene, jnp.asarray(z_matrix()), after)
+    )(part, state, jnp.asarray(z_matrix()), after)
 
 
 def merge_kernel(kept, got, after, stay, leave):
@@ -337,14 +363,17 @@
         slot = step % 2
         xs = pl.ds(GROUP * step, GROUP)
 
-        def copy_out(at):
-            return pltpu.make_async_copy(slots.at[slot], out.at[:, pl.ds(GROUP * at, GROUP)], sems.at[slot])
-
+        def copy_out(at, c):
+            return pltpu.make_async_copy(
+                slots.at[slot, c], out.at[c, pl.ds(GROUP * at, GROUP)], sems.at[slot, c]
+            )
+
+        aligned = pl.ds(pl.multiple_of(GROUP * step, GROUP), GROUP)
         @pl.when(step >= 2)
         def _():
-            copy_out(step - 2).wait()
-
-        aligned = pl.ds(pl.multiple_of(GROUP * step, GROUP), GROUP)
+            for c in range(5):
+                copy_out(step - 2, c).wait()
+
         for c in range(5):
             lines = [ghost[c, pl.ds(pl.multiple_of(32 * k + GROUP * step, 8), 8), :] for k in range(4)]
             high, low = split(jnp.concatenate(lines, axis=0))
@@ -367,6 +396,10 @@
                         value = part[c, x, rows, zs] + ql * el[c, rows, zs] + qr * er[c, rows, zs]
                         value = value + wu[0, rows, :] * low[k : k + 1]
                         value = value + wu[2, rows, :] * high[k : k + 1]
+                        if k == 0:
+                            value = value + (table[1, x] * inner[0]) * fl[5 + c, rows, zs]
+                        if k == GROUP - 1:
+                            value = value + (table[3, x] * inner[1]) * fr[5 + c, rows, zs]
                         if t == 0:
                             value = value + wu[1, rows, :] * low_edge[k : k + 1]
                         if t == 3:
@@ -376,25 +409,15 @@
                         if q == 3:
                             value = value + zpart[32 * k + 8 * t : 32 * k + 8 * t + 8, 128:]
                         slots[slot, c, k, rows, zs] = value
-
-        @pl.when(step == 0)
-        def _():
-            for c in range(5):
-                slots[slot, c, 0] = slots[slot, c, 0] + (table[1, 0] * inner[0]) * fl[5 + c]
-
-        @pl.when(step == B // GROUP - 1)
-        def _():
-            for c in range(5):
-                slots[slot, c, GROUP - 1] = slots[slot, c, GROUP - 1] + (table[3, B - 1] * inner[1]) * fr[5 + c]
-
-        copy_out(step).start()
+            copy_out(step, c).start()
         return carry
 
     lax.fori_loop(0, B // GROUP, group, 0)
     for slot in range(2):
-        pltpu.make_async_copy(
-            slots.at[slot], out.at[:, pl.ds(B - GROUP * (2 - slot), GROUP)], sems.at[slot]
-        ).wait()
+        for c in range(5):
+            pltpu.make_async_copy(
+                slots.at[slot, c], out.at[c, pl.ds(B - GROUP * (2 - slot), GROUP)], sems.at[slot, c]
+            ).wait()
 
 
 def finish(part, fl, fr, gl, gr, xr, xl, yr, yl, ghost):
@@ -408,7 +431,7 @@
         out_specs=pl.BlockSpec(memory_space=pl.ANY),
         out_shape=jax.ShapeDtypeStruct((5, B, B, NZ), F32),
         scratch_shapes=[pltpu.VMEM((5, B, NZ), F32)] * 4
-        + [pltpu.VMEM((4, B, 128), F32), pltpu.VMEM((2, 5, GROUP, B, NZ), F32), pltpu.SemaphoreType.DMA((2,))],
+        + [pltpu.VMEM((4, B, 128), F32), pltpu.VMEM((2, 5, GROUP, B, NZ), F32), pltpu.SemaphoreType.DMA((2, 5))],
         compiler_params=pltpu.CompilerParams(vmem_limit_bytes=16 << 20),
         name="add_messages",
     )(
@@ -433,69 +456,99 @@
     return lax.ppermute(array, axis, [(i, (i + by) % count) for i in range(count)])
 
 
-def rows_to_send(place_x, coarse, slot_rows, slot_times):
-    devices = jnp.arange(16, dtype=jnp.int32)
-    turn = (jnp.bitwise_xor(place_x, devices)[:, None] == devices[None, :]).astype(F32)
-    both = jnp.concatenate([slot_rows, slot_times], axis=1).astype(F32)
-    both = jnp.dot(turn, both, precision=highest)
-    rows = both[:, :128] - (256 * place_x).astype(F32)
-    weight = both[:, 128:] * 0.125
-    mine = (rows >= 0.0) & (rows < 256.0)
-    slots = jnp.arange(128)
-    before = (slots[:, None] < slots[None, :]).astype(F32)
-    rank = jnp.dot(mine.astype(F32), before, precision=highest)
-    chosen = mine[:, None, :] & (rank[:, None, :] == jnp.arange(8, dtype=F32)[None, :, None])
-    index = jnp.sum(jnp.where(chosen, rows[:, None, :], 0.0), axis=2)[:, :, None]
-    late = jnp.sum(jnp.where(chosen, weight[:, None, :], 0.0), axis=2)[:, :, None]
-    hit = index == jnp.arange(256, dtype=F32)[None, None, :]
+def choose_kernel(slots_in, times_in, coarse_in, kept, sent, pick, slots, times, coarse, sems):
+    moves = [
+        pltpu.make_async_copy(slots_in, slots, sems.at[0]),
+        pltpu.make_async_copy(times_in, times, sems.at[1]),
+        pltpu.make_async_copy(coarse_in, coarse, sems.at[2]),
+    ]
+    for move in moves:
+        move.start()
+    for move in moves:
+        move.wait()
+    place = lax.axis_index("gx")
+    rows = slots[...].astype(F32)
+    weight = times[...].astype(F32) * 0.125
+
+    def iota(shape, axis):
+        return lax.broadcasted_iota(jnp.int32, shape, axis)
+
+    def exact(a, b, dims):
+        return lax.dot_general(a, b, (dims, ((), ())), precision=highest, preferred_element_type=F32)
+
+    item = iota((128, 16), 0) // 8
+    turn = (item // 2 % 4) * 4 + (item // 8) * 2 + item % 2
+    target = (jnp.bitwise_xor(turn, place) == iota((128, 16), 1)).astype(F32)
+    begin = (256 * place).astype(F32)
+    near = rows - begin
+    mine = jnp.where((near >= 0.0) & (near < 256.0), 1.0, 0.0)
+    before = (iota((128, 128), 0) < iota((128, 128), 1)).astype(F32)
+    rank = exact(mine, before, ((1,), (0,)))
+    spread = ((1,), (0,))
+    chosen = exact(target, mine, spread) * jnp.where(
+        exact(target, rank, spread) == (iota((128, 128), 0) % 8).astype(F32), 1.0, 0.0
+    )
+    index = jnp.sum(chosen * exact(target, near, spread), axis=1, keepdims=True)
+    late = jnp.sum(chosen * exact(target, weight, spread), axis=1, keepdims=True)
+    hit = index == iota((128, 256), 1).astype(F32)
     old = jnp.where(hit, 1.0 - late, 0.0)
     new = jnp.where(hit, late, 0.0)
-    return jnp.einsum("dpr,rf->dpf", old, coarse[0], precision=highest) + jnp.einsum(
-        "dpr,rf->dpf", new, coarse[1], precision=highest
-    )
+    result = exact(old, coarse[0], ((1,), (1,))) + exact(new, coarse[1], ((1,), (1,)))
+    kept[...] = result[:64]
+    sent[...] = result[64:]
+
+    self_row = (iota((8, 16), 1) == place).astype(F32)
+    owner_row = exact(self_row, rows, spread)[0:1].astype(jnp.int32) // 256
+    self_column = (iota((16, 128), 0) == place).astype(F32)
+    owner = exact(rows, self_column, ((0,), (0,))).astype(jnp.int32) // 256
+    same = (owner == owner_row) & (iota((128, 128), 1) < iota((128, 128), 0))
+    order = jnp.sum(jnp.where(same, 1.0, 0.0), axis=1, keepdims=True)
+    turn = jnp.bitwise_xor(owner, place)
+    turn = (turn // 4) * 4 + (turn % 2) * 2 + (turn // 2) % 2
+    pick[...] = jnp.where(turn * 8 + order.astype(jnp.int32) == iota((128, 128), 1), 1.0, 0.0)
+
+
+def choose(slot_rows, slot_times, coarse):
+    return pl.pallas_call(
+        choose_kernel,
+        in_specs=[ANYWHERE] * 3,
+        out_specs=[IN_VMEM] * 3,
+        out_shape=[pltpu.VMEM((64, 160), F32)] * 2 + [pltpu.VMEM((128, 128), F32)],
+        scratch_shapes=[
+            pltpu.VMEM((16, 128), jnp.int32),
+            pltpu.VMEM((16, 128), jnp.int32),
+            pltpu.VMEM((2, 160, 256), F32),
+            pltpu.SemaphoreType.DMA((3,)),
+        ],
+        compiler_params=pltpu.CompilerParams(vmem_limit_bytes=6 << 20),
+        name="choose_rows",
+    )(*(in_hbm(a) for a in (slot_rows, slot_times, coarse)))
 
 
 def trade(sent, bit):
     return lax.ppermute(sent, "gx", [(i, i ^ bit) for i in range(16)])
 
 
-def slot_picks(place_x, slot_rows):
-    own = lax.dynamic_index_in_dim(slot_rows, place_x, 0, keepdims=False)
-    owner = own // 256
-    slots = jnp.arange(128)
-    same = (owner[:, None] == owner[None, :]) & (slots[None, :] < slots[:, None])
-    rank = jnp.sum(same.astype(jnp.int32), axis=1)
-    turn = jnp.bitwise_xor(owner, place_x)
-    order = (turn // 4) * 4 + (turn % 2) * 2 + (turn // 2) % 2
-    return (order[:, None] * 8 + rank[:, None] == slots[None, :]).astype(F32)
-
-
 def local(density, momentum, energy, coarse_rows, ghost_rows, time_index):
-    density, momentum, energy = (
-        pltpu.with_memory_space_constraint(a, pltpu.HBM) for a in (density, momentum, energy)
-    )
-    place_x = lax.axis_index("gx")
-    slot_rows = ghost_rows[0]
-    rows = rows_to_send(place_x, coarse_rows[:, :, 0, :], slot_rows, time_index[0])
-    pick = slot_picks(place_x, slot_rows)
-    rows = rows.reshape(4, 2, 2, 8, 160)
-    kept, sent = rows[:, 0].reshape(64, 160), rows[:, 1].reshape(64, 160)
-    kept, sent, pick = lax.optimization_barrier((kept, sent, pick))
+    density, momentum, energy = (in_hbm(a) for a in (density, momentum, energy))
+    cells = density, momentum, energy
+    kept, sent, pick = choose(ghost_rows[0], time_index[0], coarse_rows[:, :, 0, :].transpose(0, 2, 1))
     got = trade(sent, 2)
-    kept, sent = merge(kept, got, pick)
+    begun = y_part(0, *cells, sent)
+    kept, sent = merge(kept, got, begun[3])
     got = trade(sent, 1)
-    part, xr, xl, yr, yl = xy_part(density, momentum, energy, sent)
+    state, part, fbuf, yr, yl = y_part(2, *cells, sent, begun)
+    kept, sent = merge(kept, got, yr)
+    got = trade(sent, 4)
+    part, xr, xl = x_part(part, fbuf, sent)
     kept, sent = merge(kept, got, xr)
     xr, xl, yr, yl, sent = lax.optimization_barrier((xr, xl, yr, yl, sent))
     fl = ring(xr, "gx", 1)
     fr = ring(xl, "gx", -1)
     gl = ring(yr, "gy", 1)
     gr = ring(yl, "gy", -1)
-    got = trade(sent, 4)
-    part = z_part(0, part, density, momentum, energy, sent)
-    kept, sent = merge(kept, got, part)
     got = trade(sent, 8)
-    part = z_part(2, part, density, momentum, energy, sent)
+    part = z_part(part, state, sent)
     ghost = ghost_flux(pick, kept, got)
     return finish(part, fl, fr, gl, gr, xr, xl, yr, yl, ghost)
 

time: 73.7 us -> 58.6 us (0.80); the launches traced: 72.3 us -> 58.4 us
  matrix products: 3.55 us -> 0 us
  waiting for transfers between devices: 4.47 us -> 1.96 us
  Pallas kernels: 42.5 us -> 40.1 us
  local copies, waits for them, and re-layouts: 2.04 us -> 0.09 us
  other arithmetic: 1.87 us -> 0 us
  starting transfers between devices: 17.7 us -> 16.1 us
    dot_general x4 -> x0, matrix products: 3.55 us -> none  [the longest x1 1.26 us: rows_to_send(): jnp.einsum('dpr,rf->dpf', new, coarse[1], precision=highest)]
    ppermute x4, waiting for transfers between devices: 4.46 us -> 1.95 us  [trade(): return lax.ppermute(sent, 'gx', [(i, i ^ bit) for i in range(16)])]
    pallas_call x3 -> x5, Pallas kernels: 34.6 us -> 32.5 us  [the longest x2 16 us: y_part(): pl.pallas_call(functools.partial(y_kernel, first), in_specs=[ANYWHERE] *...]
    unnamed x10 -> x8, local copies, waits for them, and re-layouts: 1.95 us -> 0.02 us
    ppermute x4, starting transfers between devices: 9.01 us -> 8.03 us  [ring(): lax.ppermute(array, axis, [(i, (i + by) % count) for i in range(count)])]
    select_n x1 -> x0, other arithmetic: 0.76 us -> none  [slot_picks(): owner = own // 256]
  transfers between devices with their start and end apart: 8 -> 8, of which waited for: 2 -> 1; matrix products, arithmetic and copies ran while one was open for 0% -> 0% of each run, Pallas kernels for 49% -> 53%
where the time goes in v2:
time: 58.6 us; the launch traced here: 58.4 us
  Pallas kernels  40.1 us (68%)
  starting transfers between devices  16.1 us (27%)
  waiting for transfers between devices  1.96 us (3%)
    pallas_call x2, Pallas kernels, y_part(): pl.pallas_call(functools.partial(y_kernel, first), in_specs=[ANYWHERE] *...  16 us
    pallas_call x1, Pallas kernels, z_part(): pl.pallas_call(z_kernel, in_specs=[IN_VMEM] * 3 + [ANYWHERE], out_specs=I...  10.1 us
    ppermute x4, starting transfers between devices, trade(): return lax.ppermute(sent, 'gx', [(i, i ^ bit) for i in range(16)])  8.1 us
    ppermute x4, starting transfers between devices, ring(): lax.ppermute(array, axis, [(i, (i + by) % count) for i in range(count)])  8.03 us
    pallas_call x1, Pallas kernels, finish(): pl.pallas_call(finish_kernel, in_specs=[smem] + [vmem] * 12, out_specs=pl...  6.71 us
    pallas_call x1, Pallas kernels, x_part(): pl.pallas_call(x_kernel, in_specs=[IN_VMEM] * 3 + [ANYWHERE], out_specs=[...  4.16 us
    pallas_call x1, Pallas kernels, choose(): pl.pallas_call(choose_kernel, in_specs=[ANYWHERE] * 3, out_specs=[IN_VMEM...  2.22 us
    ppermute x4, waiting for transfers between devices, trade(): return lax.ppermute(sent, 'gx', [(i, i ^ bit) for i in range(16)])  1.95 us
  transfers between devices with their start and end apart: 8, of which 1 were waited for; matrix products, arithmetic and copies ran while one was open for 0% of the time, Pallas kernels for 53%

profile of v2, /device:TPU:1, one launch (start us, length us, event | category | flops | bytes accessed | tf_op | source)
XLA Modules:
  0.0 58.4 jit_solution(9907493093226947296)
XLA Ops:
  0.0 2.2 %choose_rows.1 = (f32[64,160]{1,0:T(8,128)S(1)}, f32[64,160]{1,0:T(8,128)S(1)}, f32[128,128]{1,0:T(8,128)S(1)}) custom-call(s32[16,128]{1,0:T(8,128)} %bitcast.6, s32[16,128]{1,0:T(8,128)} %bitcast.7, f32[2,160,256]{2,1,0:T(8,128)} %bitcast.5), custom_call_target="tpu_custom_call" | custom-call | tf_op jit(solution)/shard_map/choose_rows/pallas_call | solution.py:512
  2.2 3.8 %collective-permute-start = (f32[64,160]{1,0:T(8,128)S(1)}, f32[64,160]{1,0:T(8,128)S(1)}, u32[]{:S(2)}, u32[]{:S(2)}) collective-permute-start(f32[64,160]{1,0:T(8,128)S(1)} %get-tuple-element.33.refs_4_), channel_id=1, source_target_pairs={{0,16},{8,24},{16,0},{24,8},{32,48},{40,56},{48,32},{56,40},{64,80... | collective-permute-start | bytes 122888 | tf_op jit(solution)/shard_map/ppermute | solution.py:529
  6.0 8.0 %y_part.2 = (f32[5,32,32,512]{3,2,1,0:T(8,128)S(1)}, f32[5,32,32,512]{3,2,1,0:T(8,128)S(1)}, bf16[5,4,512,512]{3,2,1,0:T(8,128)(2,1)S(1)}, f32[10,32,512]{2,1,0:T(8,128)S(1)}, f32[10,32,512]{2,1,0:T(8,128)S(1)}) custom-call(f32[32,32,512]{2,1,0:T(8,128)} %refs_0_.3, f32[3,32,32,512]{3,2,1,0:T(8,128)} %refs_1_.3, f32[32,32,512]{2,1,0:T(8,128)} %refs_2_.3, ...), custom_call_target="tpu_custom_call" | custom-call | tf_op jit(solution)/shard_map/y_part/pallas_call | solution.py:196
  14.0 0.0 collective-permute-done.got
  14.1 0.5 collective-permute-start.1
  14.6 0.0 copy-start.1
  14.6 8.0 %y_part.3 = (f32[5,32,32,512]{3,2,1,0:T(8,128)S(1)}, f32[5,32,32,512]{3,2,1,0:T(8,128)S(1)}, bf16[5,4,512,512]{3,2,1,0:T(8,128)(2,1)S(1)}, f32[10,32,512]{2,1,0:T(8,128)S(1)}, f32[10,32,512]{2,1,0:T(8,128)S(1)}) custom-call(f32[32,32,512]{2,1,0:T(8,128)} %refs_0_.3, ...), custom_call_target="tpu_custom_call", output_to_operand_aliasing={{0}: (5, {}), {1}: (6, {}), {2}: (7, {}), {3}: (8, {}), {4}... | custom-call | tf_op jit(solution)/shard_map/y_part/pallas_call | solution.py:196
  22.6 0.0 collective-permute-done.1.got
  22.6 1.7 %collective-permute-start.2 = (f32[64,160]{1,0:T(8,128)S(1)}, f32[64,160]{1,0:T(8,128)S(1)}, u32[]{:S(2)}, u32[]{:S(2)}) collective-permute-start(f32[64,160]{1,0:T(8,128)S(1)} %get-tuple-element.44.after), channel_id=1, source_target_pairs={{0,32},{8,40},{16,48},{24,56},{32,0},{40,8},{48,16},{56,24},{64,96... | collective-permute-start | bytes 122888 | tf_op jit(solution)/shard_map/ppermute | solution.py:529
  24.3 0.0 copy-done.1
  24.3 0.0 copy-start
  24.3 4.2 %x_part.1 = (f32[5,32,32,512]{3,2,1,0:T(8,128)S(1)}, f32[10,32,512]{2,1,0:T(8,128)S(1)}, f32[10,32,512]{2,1,0:T(8,128)S(1)}) custom-call(f32[5,32,32,512]{3,2,1,0:T(8,128)S(1)} %get-tuple-element.40.start, bf16[5,4,512,512]{3,2,1,0:T(8,128)(2,1)S(1)} %get-tuple-element.41.fbuf, bf16[304,512]{1,0:T(8,128)(2,1)S(1)} %copy-done.1, ...), custom_call_target="tpu_custom_call", output_to_operand_aliasing={{0}: (0, {})} | custom-call | tf_op jit(solution)/shard_map/x_part/pallas_call | solution.py:234
  28.5 0.0 collective-permute-done.2.got
  28.5 1.1 %collective-permute-start.3 = (f32[10,32,512]{2,1,0:T(8,128)S(1)}, f32[10,32,512]{2,1,0:T(8,128)S(1)}, u32[]{:S(2)}, u32[]{:S(2)}) collective-permute-start(f32[10,32,512]{2,1,0:T(8,128)S(1)} %get-tuple-element.53.after.xr), channel_id=1, source_target_pairs={{0,8},{8,16},{16,24},{24,32},{32,40},{40,48},{48,56},{56,64},{64,7... | collective-permute-start | bytes 1966088 | tf_op jit(solution)/shard_map/ppermute | solution.py:456
  29.7 3.7 %collective-permute-start.4 = (f32[10,32,512]{2,1,0:T(8,128)S(1)}, f32[10,32,512]{2,1,0:T(8,128)S(1)}, u32[]{:S(2)}, u32[]{:S(2)}) collective-permute-start(f32[10,32,512]{2,1,0:T(8,128)S(1)} %get-tuple-element.54.xl), channel_id=1, source_target_pairs={{0,120},{8,0},{16,8},{24,16},{32,24},{40,32},{48,40},{56,48},{64,5... | collective-permute-start | bytes 1966088 | tf_op jit(solution)/shard_map/ppermute | solution.py:456
  33.4 3.2 %collective-permute-start.5 = (f32[10,32,512]{2,1,0:T(8,128)S(1)}, f32[10,32,512]{2,1,0:T(8,128)S(1)}, u32[]{:S(2)}, u32[]{:S(2)}) collective-permute-start(f32[10,32,512]{2,1,0:T(8,128)S(1)} %get-tuple-element.55.after.yr), channel_id=1, source_target_pairs={{0,1},{1,2},{2,3},{3,4},{4,5},{5,6},{6,7},{7,0},{8,9},{9,10},{10,1... | collective-permute-start | bytes 1966088 | tf_op jit(solution)/shard_map/ppermute | solution.py:456
  36.5 0.0 collective-permute-start.6
  36.6 2.1 %collective-permute-start.7 = (f32[64,160]{1,0:T(8,128)S(1)}, f32[64,160]{1,0:T(8,128)S(1)}, u32[]{:S(2)}, u32[]{:S(2)}) collective-permute-start(f32[64,160]{1,0:T(8,128)S(1)} %get-tuple-element.52.after), channel_id=1, source_target_pairs={{0,64},{8,72},{16,80},{24,88},{32,96},{40,104},{48,112},{56,120},{... | collective-permute-start | bytes 122888 | tf_op jit(solution)/shard_map/ppermute | solution.py:529
  38.6 0.0 copy-done
  38.6 0.0 copy-start.3
  38.6 0.0 copy-start.2
  38.6 10.1 %z_part.1.part = f32[5,32,32,512]{3,2,1,0:T(8,128)S(1)} custom-call(f32[5,32,32,512]{3,2,1,0:T(8,128)S(1)} %get-tuple-element.45.start, f32[5,32,32,512]{3,2,1,0:T(8,128)S(1)} %get-tuple-element.46.state, bf16[512,512]{1,0:T(8,128)(2,1)S(1)} %copy-done, f32[64,160]{1,0:T(8,128)S(1)} %get-tuple-element.52.after), custom_call_target="tpu_custom_call", output_to_operand_aliasing={{}: (0, {})} | custom-call | tf_op jit(solution)/shard_map/z_part/pallas_call | solution.py:280
  48.8 1.9 %collective-permute-done.7.got = f32[64,160]{1,0:T(8,128)S(1)} collective-permute-done((f32[64,160]{1,0:T(8,128)S(1)}, f32[64,160]{1,0:T(8,128)S(1)}, u32[]{:S(2)}, u32[]{:S(2)}) %collective-permute-start.7) | collective-permute-done | bytes 40992 | tf_op jit(solution)/shard_map/ppermute | solution.py:529
  50.7 0.9 %ghost_flux.1.ghost = f32[5,128,256]{2,1,0:T(8,128)S(1)} custom-call(f32[128,128]{1,0:T(8,128)S(1)} %get-tuple-element.57.pick, f32[64,160]{1,0:T(8,128)S(1)} %get-tuple-element.58.kept, f32[64,160]{1,0:T(8,128)S(1)} %collective-permute-done.7.got), custom_call_target="tpu_custom_call" | custom-call | tf_op jit(solution)/shard_map/ghost_flux/pallas_call | solution.py:323
  51.6 0.0 collective-permute-done.3.fl
  51.6 0.0 collective-permute-done.4.fr
  51.6 0.0 collective-permute-done.5.gl
  51.6 0.0 collective-permute-done.6.gr
  51.6 0.0 copy-done.3
  51.6 0.1 jit_solution_.3.wy
  51.7 0.0 copy-done.2
  51.7 6.7 %add_messages.1 = f32[5,32,32,512]{3,2,1,0:T(8,128)} custom-call(f32[4,32]{1,0:T(4,128)S(1)} %copy-done.3, f32[5,32,32,512]{3,2,1,0:T(8,128)S(1)} %z_part.1.part, f32[10,32,512]{2,1,0:T(8,128)S(1)} %collective-permute-done.3.fl, f32[10,32,512]{2,1,0:T(8,128)S(1)} %collective-permute-done.4.fr, f32[10,32,512]{2,1,0:T(8,128)S(1)} %collective-permute-done.5.gl, ...), custom_call_target="tpu_custom_call" | custom-call | tf_op jit(solution)/shard_map/add_messages/pallas_call | solution.py:428
  (3 shorter events, 0.0 us)
Async XLA Ops:
  2.2 11.8 %collective-permute-start = (f32[64,160]{1,0:T(8,128)S(1)}, f32[64,160]{1,0:T(8,128)S(1)}, u32[]{:S(2)}, u32[]{:S(2)}) collective-permute-start(f32[64,160]{1,0:T(8,128)S(1)} %get-tuple-element.33.refs_4_), channel_id=1, source_target_pairs={{0,16},{8,24},{16,0},{24,8},{32,48},{40,56},{48,32},{56,40},{64,80... | collective-permute-start | bytes 122888 | tf_op jit(solution)/shard_map/ppermute | solution.py:529
  14.1 8.5 %collective-permute-start.1 = (f32[64,160]{1,0:T(8,128)S(1)}, f32[64,160]{1,0:T(8,128)S(1)}, u32[]{:S(2)}, u32[]{:S(2)}) collective-permute-start(f32[64,160]{1,0:T(8,128)S(1)} %get-tuple-element.35.refs_4_), channel_id=1, source_target_pairs={{0,8},{8,0},{16,24},{24,16},{32,40},{40,32},{48,56},{56,48},{64,72... | collective-permute-start | bytes 122888 | tf_op jit(solution)/shard_map/ppermute | solution.py:529
  14.6 9.8 %copy-start.1 = (bf16[304,512]{1,0:T(8,128)(2,1)S(1)}, bf16[304,512]{1,0:T(8,128)(2,1)}, u32[]{:S(2)}) copy-start(bf16[304,512]{1,0:T(8,128)(2,1)} %constant.11.clone.kx) | copy-start | bytes 933892
  22.6 5.9 %collective-permute-start.2 = (f32[64,160]{1,0:T(8,128)S(1)}, f32[64,160]{1,0:T(8,128)S(1)}, u32[]{:S(2)}, u32[]{:S(2)}) collective-permute-start(f32[64,160]{1,0:T(8,128)S(1)} %get-tuple-element.44.after), channel_id=1, source_target_pairs={{0,32},{8,40},{16,48},{24,56},{32,0},{40,8},{48,16},{56,24},{64,96... | collective-permute-start | bytes 122888 | tf_op jit(solution)/shard_map/ppermute | solution.py:529
  24.3 14.3 %copy-start = (bf16[512,512]{1,0:T(8,128)(2,1)S(1)}, bf16[512,512]{1,0:T(8,128)(2,1)}, u32[]{:S(2)}) copy-start(bf16[512,512]{1,0:T(8,128)(2,1)} %constant.12.clone.mz) | copy-start | bytes 1572868
  28.5 23.1 %collective-permute-start.3 = (f32[10,32,512]{2,1,0:T(8,128)S(1)}, f32[10,32,512]{2,1,0:T(8,128)S(1)}, u32[]{:S(2)}, u32[]{:S(2)}) collective-permute-start(f32[10,32,512]{2,1,0:T(8,128)S(1)} %get-tuple-element.53.after.xr), channel_id=1, source_target_pairs={{0,8},{8,16},{16,24},{24,32},{32,40},{40,48},{48,56},{56,64},{64,7... | collective-permute-start | bytes 1966088 | tf_op jit(solution)/shard_map/ppermute | solution.py:456
  29.7 21.9 %collective-permute-start.4 = (f32[10,32,512]{2,1,0:T(8,128)S(1)}, f32[10,32,512]{2,1,0:T(8,128)S(1)}, u32[]{:S(2)}, u32[]{:S(2)}) collective-permute-start(f32[10,32,512]{2,1,0:T(8,128)S(1)} %get-tuple-element.54.xl), channel_id=1, source_target_pairs={{0,120},{8,0},{16,8},{24,16},{32,24},{40,32},{48,40},{56,48},{64,5... | collective-permute-start | bytes 1966088 | tf_op jit(solution)/shard_map/ppermute | solution.py:456
  33.4 18.2 %collective-permute-start.5 = (f32[10,32,512]{2,1,0:T(8,128)S(1)}, f32[10,32,512]{2,1,0:T(8,128)S(1)}, u32[]{:S(2)}, u32[]{:S(2)}) collective-permute-start(f32[10,32,512]{2,1,0:T(8,128)S(1)} %get-tuple-element.55.after.yr), channel_id=1, source_target_pairs={{0,1},{1,2},{2,3},{3,4},{4,5},{5,6},{6,7},{7,0},{8,9},{9,10},{10,1... | collective-permute-start | bytes 1966088 | tf_op jit(solution)/shard_map/ppermute | solution.py:456
  36.5 15.1 %collective-permute-start.6 = (f32[10,32,512]{2,1,0:T(8,128)S(1)}, f32[10,32,512]{2,1,0:T(8,128)S(1)}, u32[]{:S(2)}, u32[]{:S(2)}) collective-permute-start(f32[10,32,512]{2,1,0:T(8,128)S(1)} %get-tuple-element.56.yl), channel_id=1, source_target_pairs={{0,7},{1,0},{2,1},{3,2},{4,3},{5,4},{6,5},{7,6},{8,15},{9,8},{10,9... | collective-permute-start | bytes 1966088 | tf_op jit(solution)/shard_map/ppermute | solution.py:456
  36.6 14.2 %collective-permute-start.7 = (f32[64,160]{1,0:T(8,128)S(1)}, f32[64,160]{1,0:T(8,128)S(1)}, u32[]{:S(2)}, u32[]{:S(2)}) collective-permute-start(f32[64,160]{1,0:T(8,128)S(1)} %get-tuple-element.52.after), channel_id=1, source_target_pairs={{0,64},{8,72},{16,80},{24,88},{32,96},{40,104},{48,112},{56,120},{... | collective-permute-start | bytes 122888 | tf_op jit(solution)/shard_map/ppermute | solution.py:529
  38.6 13.0 %copy-start.3 = (f32[4,32]{1,0:T(4,128)S(1)}, f32[4,32]{1,0:T(4,128)}, u32[]{:S(2)}) copy-start(f32[4,32]{1,0:T(4,128)} %constant.13.clone.table) | copy-start | bytes 1540
  38.6 13.1 %copy-start.2 = (bf16[96,256]{1,0:T(8,128)(2,1)S(1)}, bf16[96,256]{1,0:T(8,128)(2,1)}, u32[]{:S(2)}) copy-start(bf16[96,256]{1,0:T(8,128)(2,1)} %constant.15.clone.mg) | copy-start | bytes 147460

commit v3 on v2

--- a/solution.py
+++ b/solution.py
@@ -177,6 +177,15 @@
                 copy.wait()
         if i == 1:
             matrix.wait()
+        if i == 0:
+
+            def opening(k, carry):
+                for j in range(8):
+                    piece(0, 8 * k + j, g0)
+                return carry
+
+            lax.fori_loop(0, 4, opening, 0)
+            continue
 
         def stage(c, carry, i=i):
             if i < 2:
@@ -255,8 +264,14 @@
                 row = pl.multiple_of(64 * xp + 64 * x2 + 32 * yh, 32)
                 hbuf[c, pl.ds(row, 32), zs] = h[c][32 * x2 : 32 * x2 + 32]
 
+    def opening(k, carry):
+        for j in range(8):
+            piece(0, 8 * k + j, h0)
+        return carry
+
+    lax.fori_loop(0, 4, opening, 0)
     hs = (h0, h1)
-    for i in range(5):
+    for i in range(1, 5):
 
         def stage(c, carry, i=i):
             along = []

time: 58.6 us -> 58.2 us (level)
  no operation moved by 1% of the time
where the time goes in v3:
time: 58.2 us; the launch traced here: 58.1 us
  Pallas kernels  39.6 us (68%)
  starting transfers between devices  16.1 us (28%)
  waiting for transfers between devices  2.06 us (4%)
    pallas_call x2, Pallas kernels, y_part(): pl.pallas_call(functools.partial(y_kernel, first), in_specs=[ANYWHERE] *...  15.6 us
    pallas_call x1, Pallas kernels, z_part(): pl.pallas_call(z_kernel, in_specs=[IN_VMEM] * 3 + [ANYWHERE], out_specs=I...  10 us
    ppermute x4, starting transfers between devices, trade(): return lax.ppermute(sent, 'gx', [(i, i ^ bit) for i in range(16)])  8.11 us
    ppermute x4, starting transfers between devices, ring(): lax.ppermute(array, axis, [(i, (i + by) % count) for i in range(count)])  8.03 us
    pallas_call x1, Pallas kernels, finish(): pl.pallas_call(finish_kernel, in_specs=[smem] + [vmem] * 12, out_specs=pl...  6.71 us
    pallas_call x1, Pallas kernels, x_part(): pl.pallas_call(x_kernel, in_specs=[IN_VMEM] * 3 + [ANYWHERE], out_specs=[...  4.16 us
    pallas_call x1, Pallas kernels, choose(): pl.pallas_call(choose_kernel, in_specs=[ANYWHERE] * 3, out_specs=[IN_VMEM...  2.22 us
    ppermute x4, waiting for transfers between devices, trade(): return lax.ppermute(sent, 'gx', [(i, i ^ bit) for i in range(16)])  2.05 us
  transfers between devices with their start and end apart: 8, of which 1 were waited for; matrix products, arithmetic and copies ran while one was open for 0% of the time, Pallas kernels for 53%

profile of v3, /device:TPU:1, one launch (start us, length us, event | category | flops | bytes accessed | tf_op | source)
XLA Modules:
  0.0 58.1 jit_solution(12062005291891321087)
XLA Ops:
  0.0 2.2 %choose_rows.1 = (f32[64,160]{1,0:T(8,128)S(1)}, f32[64,160]{1,0:T(8,128)S(1)}, f32[128,128]{1,0:T(8,128)S(1)}) custom-call(s32[16,128]{1,0:T(8,128)} %bitcast.6, s32[16,128]{1,0:T(8,128)} %bitcast.7, f32[2,160,256]{2,1,0:T(8,128)} %bitcast.5), custom_call_target="tpu_custom_call" | custom-call | tf_op jit(solution)/shard_map/choose_rows/pallas_call | solution.py:527
  2.2 3.8 %collective-permute-start = (f32[64,160]{1,0:T(8,128)S(1)}, f32[64,160]{1,0:T(8,128)S(1)}, u32[]{:S(2)}, u32[]{:S(2)}) collective-permute-start(f32[64,160]{1,0:T(8,128)S(1)} %get-tuple-element.33.refs_4_), channel_id=1, source_target_pairs={{0,16},{8,24},{16,0},{24,8},{32,48},{40,56},{48,32},{56,40},{64,80... | collective-permute-start | bytes 122888 | tf_op jit(solution)/shard_map/ppermute | solution.py:544
  6.0 7.8 %y_part.2 = (f32[5,32,32,512]{3,2,1,0:T(8,128)S(1)}, f32[5,32,32,512]{3,2,1,0:T(8,128)S(1)}, bf16[5,4,512,512]{3,2,1,0:T(8,128)(2,1)S(1)}, f32[10,32,512]{2,1,0:T(8,128)S(1)}, f32[10,32,512]{2,1,0:T(8,128)S(1)}) custom-call(f32[32,32,512]{2,1,0:T(8,128)} %refs_0_.3, f32[3,32,32,512]{3,2,1,0:T(8,128)} %refs_1_.3, f32[32,32,512]{2,1,0:T(8,128)} %refs_2_.3, ...), custom_call_target="tpu_custom_call" | custom-call | tf_op jit(solution)/shard_map/y_part/pallas_call | solution.py:205
  13.8 0.0 collective-permute-done.got
  13.9 0.5 collective-permute-start.1
  14.4 0.0 copy-start.1
  14.4 7.8 %y_part.3 = (f32[5,32,32,512]{3,2,1,0:T(8,128)S(1)}, f32[5,32,32,512]{3,2,1,0:T(8,128)S(1)}, bf16[5,4,512,512]{3,2,1,0:T(8,128)(2,1)S(1)}, f32[10,32,512]{2,1,0:T(8,128)S(1)}, f32[10,32,512]{2,1,0:T(8,128)S(1)}) custom-call(f32[32,32,512]{2,1,0:T(8,128)} %refs_0_.3, ...), custom_call_target="tpu_custom_call", output_to_operand_aliasing={{0}: (5, {}), {1}: (6, {}), {2}: (7, {}), {3}: (8, {}), {4}... | custom-call | tf_op jit(solution)/shard_map/y_part/pallas_call | solution.py:205
  22.2 0.0 collective-permute-done.1.got
  22.2 1.7 %collective-permute-start.2 = (f32[64,160]{1,0:T(8,128)S(1)}, f32[64,160]{1,0:T(8,128)S(1)}, u32[]{:S(2)}, u32[]{:S(2)}) collective-permute-start(f32[64,160]{1,0:T(8,128)S(1)} %get-tuple-element.44.after), channel_id=1, source_target_pairs={{0,32},{8,40},{16,48},{24,56},{32,0},{40,8},{48,16},{56,24},{64,96... | collective-permute-start | bytes 122888 | tf_op jit(solution)/shard_map/ppermute | solution.py:544
  24.0 0.0 copy-done.1
  24.0 0.0 copy-start
  24.0 4.2 %x_part.1 = (f32[5,32,32,512]{3,2,1,0:T(8,128)S(1)}, f32[10,32,512]{2,1,0:T(8,128)S(1)}, f32[10,32,512]{2,1,0:T(8,128)S(1)}) custom-call(f32[5,32,32,512]{3,2,1,0:T(8,128)S(1)} %get-tuple-element.40.start, bf16[5,4,512,512]{3,2,1,0:T(8,128)(2,1)S(1)} %get-tuple-element.41.fbuf, bf16[304,512]{1,0:T(8,128)(2,1)S(1)} %copy-done.1, ...), custom_call_target="tpu_custom_call", output_to_operand_aliasing={{0}: (0, {})} | custom-call | tf_op jit(solution)/shard_map/x_part/pallas_call | solution.py:243
  28.1 0.0 collective-permute-done.2.got
  28.1 1.1 %collective-permute-start.3 = (f32[10,32,512]{2,1,0:T(8,128)S(1)}, f32[10,32,512]{2,1,0:T(8,128)S(1)}, u32[]{:S(2)}, u32[]{:S(2)}) collective-permute-start(f32[10,32,512]{2,1,0:T(8,128)S(1)} %get-tuple-element.53.after.xr), channel_id=1, source_target_pairs={{0,8},{8,16},{16,24},{24,32},{32,40},{40,48},{48,56},{56,64},{64,7... | collective-permute-start | bytes 1966088 | tf_op jit(solution)/shard_map/ppermute | solution.py:471
  29.3 3.7 %collective-permute-start.4 = (f32[10,32,512]{2,1,0:T(8,128)S(1)}, f32[10,32,512]{2,1,0:T(8,128)S(1)}, u32[]{:S(2)}, u32[]{:S(2)}) collective-permute-start(f32[10,32,512]{2,1,0:T(8,128)S(1)} %get-tuple-element.54.xl), channel_id=1, source_target_pairs={{0,120},{8,0},{16,8},{24,16},{32,24},{40,32},{48,40},{56,48},{64,5... | collective-permute-start | bytes 1966088 | tf_op jit(solution)/shard_map/ppermute | solution.py:471
  33.0 3.2 %collective-permute-start.5 = (f32[10,32,512]{2,1,0:T(8,128)S(1)}, f32[10,32,512]{2,1,0:T(8,128)S(1)}, u32[]{:S(2)}, u32[]{:S(2)}) collective-permute-start(f32[10,32,512]{2,1,0:T(8,128)S(1)} %get-tuple-element.55.after.yr), channel_id=1, source_target_pairs={{0,1},{1,2},{2,3},{3,4},{4,5},{5,6},{6,7},{7,0},{8,9},{9,10},{10,1... | collective-permute-start | bytes 1966088 | tf_op jit(solution)/shard_map/ppermute | solution.py:471
  36.2 0.0 collective-permute-start.6
  36.2 2.1 %collective-permute-start.7 = (f32[64,160]{1,0:T(8,128)S(1)}, f32[64,160]{1,0:T(8,128)S(1)}, u32[]{:S(2)}, u32[]{:S(2)}) collective-permute-start(f32[64,160]{1,0:T(8,128)S(1)} %get-tuple-element.52.after), channel_id=1, source_target_pairs={{0,64},{8,72},{16,80},{24,88},{32,96},{40,104},{48,112},{56,120},{... | collective-permute-start | bytes 122888 | tf_op jit(solution)/shard_map/ppermute | solution.py:544
  38.3 0.0 copy-done
  38.3 0.0 copy-start.3
  38.3 0.0 copy-start.2
  38.3 10.0 %z_part.1.part = f32[5,32,32,512]{3,2,1,0:T(8,128)S(1)} custom-call(f32[5,32,32,512]{3,2,1,0:T(8,128)S(1)} %get-tuple-element.45.start, f32[5,32,32,512]{3,2,1,0:T(8,128)S(1)} %get-tuple-element.46.state, bf16[512,512]{1,0:T(8,128)(2,1)S(1)} %copy-done, f32[64,160]{1,0:T(8,128)S(1)} %get-tuple-element.52.after), custom_call_target="tpu_custom_call", output_to_operand_aliasing={{}: (0, {})} | custom-call | tf_op jit(solution)/shard_map/z_part/pallas_call | solution.py:295
  48.3 2.0 %collective-permute-done.7.got = f32[64,160]{1,0:T(8,128)S(1)} collective-permute-done((f32[64,160]{1,0:T(8,128)S(1)}, f32[64,160]{1,0:T(8,128)S(1)}, u32[]{:S(2)}, u32[]{:S(2)}) %collective-permute-start.7) | collective-permute-done | bytes 40992 | tf_op jit(solution)/shard_map/ppermute | solution.py:544
  50.3 0.9 %ghost_flux.1.ghost = f32[5,128,256]{2,1,0:T(8,128)S(1)} custom-call(f32[128,128]{1,0:T(8,128)S(1)} %get-tuple-element.57.pick, f32[64,160]{1,0:T(8,128)S(1)} %get-tuple-element.58.kept, f32[64,160]{1,0:T(8,128)S(1)} %collective-permute-done.7.got), custom_call_target="tpu_custom_call" | custom-call | tf_op jit(solution)/shard_map/ghost_flux/pallas_call | solution.py:338
  51.2 0.0 collective-permute-done.3.fl
  51.2 0.0 collective-permute-done.4.fr
  51.2 0.0 collective-permute-done.5.gl
  51.2 0.0 collective-permute-done.6.gr
  51.3 0.0 copy-done.3
  51.3 0.1 jit_solution_.3.wy
  51.3 0.0 copy-done.2
  51.4 6.7 %add_messages.1 = f32[5,32,32,512]{3,2,1,0:T(8,128)} custom-call(f32[4,32]{1,0:T(4,128)S(1)} %copy-done.3, f32[5,32,32,512]{3,2,1,0:T(8,128)S(1)} %z_part.1.part, f32[10,32,512]{2,1,0:T(8,128)S(1)} %collective-permute-done.3.fl, f32[10,32,512]{2,1,0:T(8,128)S(1)} %collective-permute-done.4.fr, f32[10,32,512]{2,1,0:T(8,128)S(1)} %collective-permute-done.5.gl, ...), custom_call_target="tpu_custom_call" | custom-call | tf_op jit(solution)/shard_map/add_messages/pallas_call | solution.py:443
  (3 shorter events, 0.0 us)
Async XLA Ops:
  2.2 11.6 %collective-permute-start = (f32[64,160]{1,0:T(8,128)S(1)}, f32[64,160]{1,0:T(8,128)S(1)}, u32[]{:S(2)}, u32[]{:S(2)}) collective-permute-start(f32[64,160]{1,0:T(8,128)S(1)} %get-tuple-element.33.refs_4_), channel_id=1, source_target_pairs={{0,16},{8,24},{16,0},{24,8},{32,48},{40,56},{48,32},{56,40},{64,80... | collective-permute-start | bytes 122888 | tf_op jit(solution)/shard_map/ppermute | solution.py:544
  13.9 8.3 %collective-permute-start.1 = (f32[64,160]{1,0:T(8,128)S(1)}, f32[64,160]{1,0:T(8,128)S(1)}, u32[]{:S(2)}, u32[]{:S(2)}) collective-permute-start(f32[64,160]{1,0:T(8,128)S(1)} %get-tuple-element.35.refs_4_), channel_id=1, source_target_pairs={{0,8},{8,0},{16,24},{24,16},{32,40},{40,32},{48,56},{56,48},{64,72... | collective-permute-start | bytes 122888 | tf_op jit(solution)/shard_map/ppermute | solution.py:544
  14.4 9.6 %copy-start.1 = (bf16[304,512]{1,0:T(8,128)(2,1)S(1)}, bf16[304,512]{1,0:T(8,128)(2,1)}, u32[]{:S(2)}) copy-start(bf16[304,512]{1,0:T(8,128)(2,1)} %constant.11.clone.kx) | copy-start | bytes 933892
  22.2 5.9 %collective-permute-start.2 = (f32[64,160]{1,0:T(8,128)S(1)}, f32[64,160]{1,0:T(8,128)S(1)}, u32[]{:S(2)}, u32[]{:S(2)}) collective-permute-start(f32[64,160]{1,0:T(8,128)S(1)} %get-tuple-element.44.after), channel_id=1, source_target_pairs={{0,32},{8,40},{16,48},{24,56},{32,0},{40,8},{48,16},{56,24},{64,96... | collective-permute-start | bytes 122888 | tf_op jit(solution)/shard_map/ppermute | solution.py:544
  24.0 14.3 %copy-start = (bf16[512,512]{1,0:T(8,128)(2,1)S(1)}, bf16[512,512]{1,0:T(8,128)(2,1)}, u32[]{:S(2)}) copy-start(bf16[512,512]{1,0:T(8,128)(2,1)} %constant.12.clone.mz) | copy-start | bytes 1572868
  28.1 23.1 %collective-permute-start.3 = (f32[10,32,512]{2,1,0:T(8,128)S(1)}, f32[10,32,512]{2,1,0:T(8,128)S(1)}, u32[]{:S(2)}, u32[]{:S(2)}) collective-permute-start(f32[10,32,512]{2,1,0:T(8,128)S(1)} %get-tuple-element.53.after.xr), channel_id=1, source_target_pairs={{0,8},{8,16},{16,24},{24,32},{32,40},{40,48},{48,56},{56,64},{64,7... | collective-permute-start | bytes 1966088 | tf_op jit(solution)/shard_map/ppermute | solution.py:471
  29.3 21.9 %collective-permute-start.4 = (f32[10,32,512]{2,1,0:T(8,128)S(1)}, f32[10,32,512]{2,1,0:T(8,128)S(1)}, u32[]{:S(2)}, u32[]{:S(2)}) collective-permute-start(f32[10,32,512]{2,1,0:T(8,128)S(1)} %get-tuple-element.54.xl), channel_id=1, source_target_pairs={{0,120},{8,0},{16,8},{24,16},{32,24},{40,32},{48,40},{56,48},{64,5... | collective-permute-start | bytes 1966088 | tf_op jit(solution)/shard_map/ppermute | solution.py:471
  33.0 18.2 %collective-permute-start.5 = (f32[10,32,512]{2,1,0:T(8,128)S(1)}, f32[10,32,512]{2,1,0:T(8,128)S(1)}, u32[]{:S(2)}, u32[]{:S(2)}) collective-permute-start(f32[10,32,512]{2,1,0:T(8,128)S(1)} %get-tuple-element.55.after.yr), channel_id=1, source_target_pairs={{0,1},{1,2},{2,3},{3,4},{4,5},{5,6},{6,7},{7,0},{8,9},{9,10},{10,1... | collective-permute-start | bytes 1966088 | tf_op jit(solution)/shard_map/ppermute | solution.py:471
  36.2 15.1 %collective-permute-start.6 = (f32[10,32,512]{2,1,0:T(8,128)S(1)}, f32[10,32,512]{2,1,0:T(8,128)S(1)}, u32[]{:S(2)}, u32[]{:S(2)}) collective-permute-start(f32[10,32,512]{2,1,0:T(8,128)S(1)} %get-tuple-element.56.yl), channel_id=1, source_target_pairs={{0,7},{1,0},{2,1},{3,2},{4,3},{5,4},{6,5},{7,6},{8,15},{9,8},{10,9... | collective-permute-start | bytes 1966088 | tf_op jit(solution)/shard_map/ppermute | solution.py:471
  36.2 14.2 %collective-permute-start.7 = (f32[64,160]{1,0:T(8,128)S(1)}, f32[64,160]{1,0:T(8,128)S(1)}, u32[]{:S(2)}, u32[]{:S(2)}) collective-permute-start(f32[64,160]{1,0:T(8,128)S(1)} %get-tuple-element.52.after), channel_id=1, source_target_pairs={{0,64},{8,72},{16,80},{24,88},{32,96},{40,104},{48,112},{56,120},{... | collective-permute-start | bytes 122888 | tf_op jit(solution)/shard_map/ppermute | solution.py:544
  38.3 13.0 %copy-start.3 = (f32[4,32]{1,0:T(4,128)S(1)}, f32[4,32]{1,0:T(4,128)}, u32[]{:S(2)}) copy-start(f32[4,32]{1,0:T(4,128)} %constant.13.clone.table) | copy-start | bytes 1540
  38.3 13.1 %copy-start.2 = (bf16[96,256]{1,0:T(8,128)(2,1)S(1)}, bf16[96,256]{1,0:T(8,128)(2,1)}, u32[]{:S(2)}) copy-start(bf16[96,256]{1,0:T(8,128)(2,1)} %constant.15.clone.mg) | copy-start | bytes 147460
